TPU v7x, 256 devices: a whole 4x4x8 slice. The times are simulated.
256 devices in a mesh: front: 64 (over x_lo, y, z), pair: 4 (over x_hi, core).
Axes of the slice: x: 4 (x_hi: 2, x_lo: 2; x = x_hi * 2 + x_lo), y: 4, z: 8, core: 2. Of those that a mesh axis runs over, the one named last changes fastest.
Arguments:
- pivot_block: float32 [64, 768, 768], P('front', 'pair'), may hold values from -1 to 8, as said below
- coupling_rows: float32 [64, 2304, 768], P('front', 'pair'), may hold values from -0.6 to 0.6
- trailing_block: float32 [64, 2304, 2304], P('front', 'pair'), may hold values from -6 to 6
- index_map: int32 [64, 2304], replicated, may hold values from 0 to 3071, as said below
Outputs:
- panel_factor: float32 [64, 2304, 768], P('front', 'pair')
- parent_front: float32 [3072, 64, 768], P('pair', 'front')
Inputs may be any that keep to these rules, and one draw needn't show every extreme that they name: pivot_block[c] is symmetric positive definite. For each child c and row block p, the entries index_map[c, p * 576 + a] for a below 576 are distinct, rising, and lie in p * 768 to (p + 1) * 768 - 1.
All inputs are finite; a program needn't handle non-finite values.
Results may differ from a plain program's by a relative error of at most 0.0029.
Values may be sent and summed in bfloat16 or wider, within the bound.
No kernel may reach another device: no remote copies, remote signals or barrier semaphores. Data moves between devices by JAX's collectives and lax.ppermute only.
A program may use at most 128 MiB of HBM per device.

v0:
```python
import functools

import jax
import jax.numpy as jnp
from jax import lax
from jax.experimental import pallas as pl
from jax.experimental.pallas import tpu as pltpu
from jax.sharding import PartitionSpec as P


PO = 3072
LEAF = 128
F32 = jnp.float32
BF16 = jnp.bfloat16


def xor_permute(value, axis, bits):
    return lax.ppermute(value, axis, [(i, i ^ bits) for i in range(lax.axis_size(axis))])


def gather_pair(block):
    far = xor_permute(block, "pair", 2)
    near = xor_permute(block, "pair", 1)
    cross = xor_permute(far, "pair", 1)
    return block, near, far, cross


def gather_pivot(block, pair_id):
    half = block.shape[1] // 2
    quadrant = lax.dynamic_slice_in_dim(block, pair_id // 2 * half, half, 1)
    far = xor_permute(quadrant, "pair", 2)
    near = xor_permute(block, "pair", 1)
    cross = xor_permute(far, "pair", 1)
    return block, near, far, cross


def halves(value):
    high = value.astype(BF16)
    return high, (value - high.astype(F32)).astype(BF16)


def in_hbm(value):
    return pltpu.with_memory_space_constraint(value, pltpu.MemorySpace.HBM)


VMEM = pl.BlockSpec(memory_space=pltpu.VMEM)
HBM = pl.BlockSpec(memory_space=pltpu.MemorySpace.HBM)


def lane_wide(value, lane):
    lanes = jnp.full((8, LEAF), lane, jnp.int32)
    return jnp.take_along_axis(value, lanes, axis=1, mode="promise_in_bounds")


def columns(groups, lane0):
    return [[lane_wide(group[0], lane0 + k) for k in range(8)] for group in groups]


def row_wide(value, row):
    return jnp.broadcast_to(value[row : row + 1, :], (8, LEAF))


def eliminate(groups, here, after, sub):
    diag, unit = groups[0]
    rest = list(groups[1:])
    cols, below = here[0], here[1:]
    scale = None
    for k in range(8):
        pivot = row_wide(cols[k], k)
        inverse = 1.0 / pivot
        root = lax.rsqrt(pivot)
        scale = root if scale is None else jnp.where(sub == k, root, scale)
        diag_row, unit_row = row_wide(diag, k), row_wide(unit, k)
        factor = jnp.where(sub > k, cols[k] * inverse, 0.0)
        others = [one[k] * inverse for one in below]
        for m in range(k + 1, 8):
            entry = row_wide(cols[m], k)
            cols[m] = cols[m] - factor * entry
            for one, other in zip(below, others):
                one[m] = one[m] - other * entry
        if after:
            for m in range(8):
                entry = row_wide(after[0][m], k)
                for one, other in zip(after, [factor] + others):
                    one[m] = one[m] - other * entry
        diag = diag - factor * diag_row
        unit = unit - factor * unit_row
        rest = [
            (one - other * diag_row, two - other * unit_row)
            for (one, two), other in zip(rest, others)
        ]
    return diag * scale, unit * scale, rest


def factor_leaf(d_ref, x_ref):
    sub = lax.broadcasted_iota(jnp.int32, (8, LEAF), 0)
    x_ref[...] = (
        lax.broadcasted_iota(jnp.int32, (LEAF, LEAF), 0)
        == lax.broadcasted_iota(jnp.int32, (LEAF, LEAF), 1)
    ).astype(F32)
    for start in range(0, LEAF, 32):
        groups = [
            (d_ref[start + g : start + g + 8, :], x_ref[start + g : start + g + 8, :])
            for g in range(0, 32, 8)
        ]
        uppers, inverses = [], []
        here = columns(groups, start)
        for g in range(0, 32, 8):
            after = columns(groups[:2], start + g + 8) if g < 24 else []
            upper, inverse, groups = eliminate(groups, here, after, sub)
            here = after[1:] + columns(groups[1:], start + g + 8) if g < 24 else []
            uppers.append(upper)
            inverses.append(inverse)
        upper, inverse = jnp.concatenate(uppers, 0), jnp.concatenate(inverses, 0)
        x_ref[start : start + 32, :] = inverse
        row = start + 32
        if row < LEAF:
            high, low = halves(upper)
            left = jnp.concatenate([high, high, low], 0)
            right = right_three(jnp.concatenate([upper, inverse], 1))
            change = lax.dot_general(
                left, right, (((0,), (0,)), ((), ())), preferred_element_type=F32
            )
            d_ref[row:, :] = d_ref[row:, :] - change[row:, :LEAF]
            x_ref[row:, :] = x_ref[row:, :] - change[row:, LEAF:]


def right_three(value):
    high, low = halves(value)
    return jnp.concatenate([high, low, high], 0)


def three(left, right):
    dot = functools.partial(jnp.dot, preferred_element_type=F32)
    return dot(left[0], right[0]) + (dot(left[0], right[1]) + dot(left[1], right[0]))


def span(first, last):
    return slice(first * LEAF, last * LEAF)


class Columns:
    def __init__(self, pieces, axis):
        self.pieces, self.axis = pieces, axis

    def _where(self, k):
        for leaves, refs in self.pieces:
            if k in leaves:
                return refs, k - leaves[0]

    def get(self, count, other):
        out = []
        for half in range(2):
            parts = []
            for leaves, refs in self.pieces:
                size = min(count, leaves[-1] + 1) - leaves[0]
                if size > 0:
                    at = span(0, size)
                    parts.append(refs[half][(at, other) if self.axis == 0 else (other, at)])
            out.append(jnp.concatenate(parts, self.axis))
        return out

    def put(self, k, other, value):
        refs, slot = self._where(k)
        at = span(slot, slot + 1)
        index = (at, other) if self.axis == 0 else (other, at)
        refs[0][index], refs[1][index] = halves(value)


def stage_kernel(stages, index, blocks, *refs):
    leaves = stages[index]
    keep = leaves[0] + 1 < blocks
    n_out = 7 if keep else 3
    if index == 0:
        own, near, far, cross, c_hbm = refs[:5]
        outs = refs[5 : 5 + n_out + 3]
        d_ref, x_ref, sems = refs[5 + n_out + 3 :]
        a_ref, c_ref, inverse_ref = outs[n_out:]
        pair_id = lax.axis_index("pair")
        rows = own.shape[0]

        def at(bits):
            return pl.ds(pl.multiple_of((pair_id ^ bits) * rows, 64), rows)

        own_copy = pltpu.make_async_copy(own, a_ref.at[at(0)], sems.at[0])
        own_copy.start()
        coupling_copy = pltpu.make_async_copy(c_hbm, c_ref, sems.at[1])
        coupling_copy.start()
        half = blocks // 2
        width = half * LEAF
        there = pl.ds(pl.multiple_of((1 - pair_id // 2) * width, LEAF), width)
        a_ref[at(1), :] = near[...]
        a_ref[at(2), there] = far[...]
        a_ref[at(3), there] = cross[...]
        own_copy.wait()

        @pl.when(pair_id >= 2)
        def _():
            for i in range(half, blocks):
                for j in range(half):
                    low, high = span(i, i + 1), span(j, j + 1)
                    a_ref[high, low] = a_ref[low, high].T

        earlier = []
    else:
        a_ref, c_ref = refs[:2]
        earlier = refs[2 : 2 + 6 * index]
        outs = refs[2 + 6 * index : 2 + 6 * index + n_out]
        d_ref, x_ref = refs[2 + 6 * index + n_out :]
    uppers, lowers, panels = [], [], []
    for i in range(index):
        p_high, p_low, u_high, u_low, l_high, l_low = earlier[6 * i : 6 * i + 6]
        panels.append((stages[i], (p_high, p_low)))
        uppers.append((stages[i], (u_high, u_low)))
        lowers.append((stages[i], (l_high, l_low)))
    panel_ref, p_high, p_low = outs[:3]
    panels.append((leaves, (p_high, p_low)))
    if keep:
        uppers.append((leaves, outs[3:5]))
        lowers.append((leaves, outs[5:7]))
    uppers, lowers, panels = Columns(uppers, 0), Columns(lowers, 1), Columns(panels, 1)
    every = slice(None)
    for slot, k in enumerate(leaves):
        here, rest = span(k, k + 1), span(k + 1, blocks)
        diag = a_ref[here, here]
        if k:
            diag = diag - three(lowers.get(k, here), uppers.get(k, here))
        d_ref[slot] = diag
        side = None
        if k and k + 1 < blocks:
            side = a_ref[here, rest] - three(lowers.get(k, here), uppers.get(k, rest))
        elif k + 1 < blocks:
            side = a_ref[here, rest]
        if k:
            coupled = c_ref[:, here] - three(panels.get(k, every), uppers.get(k, here))
        factor_leaf(d_ref.at[slot], x_ref.at[slot])
        inverse = x_ref[slot]
        if index == 0:
            inverse_ref[slot] = inverse
        if k == 0:
            coupling_copy.wait()
            coupled = c_ref[:, here]
        if side is not None:
            upper = three(halves(inverse), halves(side))
            uppers.put(k, rest, upper)
            for j in range(k + 1, blocks):
                lowers.put(k, span(j, j + 1), upper[:, span(j - k - 1, j - k)].T)
        panel = three(halves(coupled), halves(inverse.T))
        panel_ref[:, span(slot, slot + 1)] = panel
        panels.put(k, every, panel)


def stage(stages, index, blocks, operands, upd_rows, piv):
    width = len(stages[index]) * LEAF
    first, keep = index == 0, stages[index][0] + 1 < blocks
    shapes = [((upd_rows, width), F32)] + [((upd_rows, width), BF16)] * 2
    if keep:
        shapes += [((width, piv), BF16)] * 2 + [((piv, width), BF16)] * 2
    scratch = [pltpu.VMEM((len(stages[index]), LEAF, LEAF), F32)] * 2
    in_specs = [VMEM] * len(operands)
    if first:
        shapes += [((piv, piv), F32), ((upd_rows, piv), F32)]
        shapes += [((len(stages[0]), LEAF, LEAF), F32)]
        scratch.append(pltpu.SemaphoreType.DMA((2,)))
        in_specs = [HBM, VMEM, VMEM, VMEM, HBM]
        operands = [in_hbm(operands[0]), *operands[1:4], in_hbm(operands[4])]
    return pl.pallas_call(
        functools.partial(stage_kernel, stages, index, blocks),
        out_shape=[jax.ShapeDtypeStruct(*shape) for shape in shapes],
        in_specs=in_specs,
        out_specs=[VMEM] * len(shapes),
        scratch_shapes=scratch,
        cost_estimate=pl.CostEstimate(
            flops=len(stages[index]) * 2000000000, bytes_accessed=1 << 20, transcendentals=0
        ),
        compiler_params=pltpu.CompilerParams(vmem_limit_bytes=20 << 20),
    )(*operands)


def run_stages(parts, coupling, after_stage):
    upd_rows, piv = coupling.shape
    blocks = piv // LEAF
    columns, operands, base, earlier = [], [*parts, coupling], None, []
    for index in range(len(STAGES)):
        outs = stage(STAGES, index, blocks, operands, upd_rows, piv)
        columns.append(outs[0])
        after_stage(index, outs)
        if index == 0:
            base = outs[7:9]
        earlier += outs[1:7]
        operands = [*base, *earlier]
    return columns


STAGES = ((0, 1), (2, 3), (4, 5))


LATE = 1


def place_panels(sources, all_ref, at):
    pair_id = lax.axis_index("pair")
    width = sources[0].shape[1]
    for bits, source in enumerate(sources):
        all_ref[pair_id ^ bits, :, at : at + width] = source[...]


def gram(left, right):
    return lax.dot_general(left, right, (((1,), (1,)), ((), ())), preferred_element_type=F32)


def partial_kernel(own_block, *refs):
    t_ref, own_ref, near, far, cross, inverse_ref, u_high, u_low, *sources, w_ref, all_ref = refs
    pair_id = lax.axis_index("pair")
    width = own_ref.shape[1]
    all_ref[pair_id, :, :width] = own_ref[...]
    first, second = inverse_ref[0].T, inverse_ref[1].T
    at = span(0, 1), span(1, 2)
    corner = three(halves(three(halves(first), (u_high[at], u_low[at]))), halves(second))
    whole = jnp.concatenate([first, -corner], 1), jnp.concatenate([0.0 * second, second], 1)
    whole = halves(jnp.concatenate(whole, 0))
    tile = own_ref.shape[0] // 4

    def panel_rows(i, _):
        rows = pl.ds(pl.multiple_of(i * tile, 16), tile)
        for bits, early in ((1, near), (2, far), (3, cross)):
            panel = three(halves(early[rows, :]), whole)
            all_ref[pair_id ^ bits, rows, :width] = panel.astype(BF16)
        return 0

    lax.fori_loop(0, 4, panel_rows, 0)
    at = width
    for chunk in range(len(sources) // 4):
        four = sources[4 * chunk : 4 * chunk + 4]
        place_panels(four, all_ref, at)
        at += four[0].shape[1]
    sibling = lax.rem(lax.axis_index("front"), 4)
    upd_rows = t_ref.shape[0]

    def rows_of(i, _):
        rows = pl.ds(pl.multiple_of(i * tile, 16), tile)
        own = [own_ref[rows, :]] + [sources[i][rows, :] for i in range(0, len(sources), 4)]
        own = jnp.concatenate(own, 1)
        for column in range(4):

            @pl.when((sibling == column) == own_block)
            def _():
                trailing = t_ref[rows, column * upd_rows : (column + 1) * upd_rows]
                w_ref[sibling ^ column, rows, :] = trailing - gram(own, all_ref[column])

        return 0

    lax.fori_loop(0, 4, rows_of, 0)


def partial_update(trailing, first, early, chunks, own_block):
    upd_rows = trailing.shape[0]
    width = first[1].shape[1] + sum(chunk[0].shape[1] for chunk in chunks)
    start = [trailing, first[1], *early[1:], first[9], first[3], first[4]]
    sources = [source for chunk in chunks for source in chunk]
    return pl.pallas_call(
        functools.partial(partial_kernel, own_block),
        out_shape=jax.ShapeDtypeStruct((4, upd_rows, upd_rows), F32),
        in_specs=[VMEM] * (len(start) + len(sources)),
        out_specs=VMEM,
        scratch_shapes=[pltpu.VMEM((4, upd_rows, width), BF16)],
        cost_estimate=pl.CostEstimate(flops=8000000000, bytes_accessed=1 << 20, transcendentals=0),
        compiler_params=pltpu.CompilerParams(vmem_limit_bytes=24 << 20),
    )(*start, *sources)


def finish_kernel(bits, n_sources, w_ref, *refs):
    sources, refs = refs[:n_sources], refs[n_sources:]
    copies = []
    if bits == 0:
        columns, (u_ref, f_ref, all_ref, sems) = refs[:-4], refs[-4:]
        at = 0
        for i, column in enumerate(columns):
            width = column.shape[1]
            copies.append(pltpu.make_async_copy(column, f_ref.at[:, at : at + width], sems.at[i]))
            copies[-1].start()
            at += width
    else:
        u_ref, all_ref = refs
    at = 0
    for first in range(0, n_sources, 4):
        place_panels(sources[first : first + 4], all_ref, at)
        at += sources[first].shape[1]
    own = jnp.concatenate([sources[i][...] for i in range(0, n_sources, 4)], 1)
    sibling = lax.rem(lax.axis_index("front"), 4)
    u_ref[...] = (w_ref[bits] - gram(own, all_ref[sibling ^ bits])).astype(BF16)
    for copy in copies:
        copy.wait()


def finish_update(partial, chunks, bits, columns=()):
    upd_rows = partial.shape[1]
    sources = [source for chunk in chunks for source in chunk]
    width = sum(chunk[0].shape[1] for chunk in chunks)
    shapes = [jax.ShapeDtypeStruct((upd_rows, upd_rows), BF16)]
    out_specs = [VMEM]
    scratch = [pltpu.VMEM((4, upd_rows, width), BF16)]
    if columns:
        piv = sum(column.shape[1] for column in columns)
        shapes.append(jax.ShapeDtypeStruct((upd_rows, piv), F32))
        out_specs.append(HBM)
        scratch.append(pltpu.SemaphoreType.DMA((len(columns),)))
    return pl.pallas_call(
        functools.partial(finish_kernel, bits, len(sources)),
        out_shape=shapes,
        in_specs=[VMEM] * (1 + len(sources) + len(columns)),
        out_specs=out_specs,
        scratch_shapes=scratch,
        cost_estimate=pl.CostEstimate(flops=500000000, bytes_accessed=1 << 20, transcendentals=0),
        compiler_params=pltpu.CompilerParams(vmem_limit_bytes=12 << 20),
    )(partial, *sources, *columns)


def hot_block(map_ref, block, upd_rows):
    low = max(0, (block - 2) * LEAF)
    high = min((block + 1) * LEAF, upd_rows)
    rows = lax.broadcasted_iota(jnp.int32, (LEAF, high - low), 0) + block * LEAF
    return (rows == map_ref[:, low:high]).astype(F32).astype(BF16), low, high


def extend_kernel(first, last, *refs):
    part_ref, row_ref, col_ref = refs[:3]
    refs = refs[3:]
    if not first:
        sum_ref, refs = refs[0], refs[1:]
    if last:
        out_ref, moved_ref, flat_ref, sems = refs
    else:
        out_ref, moved_ref = refs
    upd_rows = part_ref.shape[0]
    blocks = moved_ref.shape[1] // LEAF
    for j in range(blocks):
        hot, low, high = hot_block(col_ref, j, upd_rows)
        moved_ref[:, j * LEAF : (j + 1) * LEAF] = lax.dot_general(
            part_ref[:, low:high], hot, (((1,), (1,)), ((), ())), preferred_element_type=F32
        ).astype(BF16)
    copies = []
    for i in range(blocks):
        rows = slice(i * LEAF, (i + 1) * LEAF)
        hot, low, high = hot_block(row_ref, i, upd_rows)
        value = jnp.dot(hot, moved_ref[low:high, :], preferred_element_type=F32)
        if not first:
            value = value + sum_ref[rows, :]
        if last:
            flat_ref[rows, 0, :] = value
            copy = pltpu.make_async_copy(flat_ref.at[rows], out_ref.at[rows], sems.at[i])
            copy.start()
            copies.append(copy)
        else:
            out_ref[rows, :] = value
    for copy in copies:
        copy.wait()


def extend_add(total, part, row_map, col_map, par_rows, last):
    first = total is None
    upd_rows = part.shape[0]
    scratch = [pltpu.VMEM((upd_rows, par_rows), BF16)]
    shape, out_specs = (par_rows, par_rows), pl.BlockSpec(memory_space=pltpu.VMEM)
    if last:
        shape, out_specs = (par_rows, 1, par_rows), HBM
        scratch += [
            pltpu.VMEM((par_rows, 1, par_rows), F32),
            pltpu.SemaphoreType.DMA((par_rows // LEAF,)),
        ]
    operands = [part, row_map, col_map] + ([] if first else [total])
    return pl.pallas_call(
        functools.partial(extend_kernel, first, last),
        out_shape=jax.ShapeDtypeStruct(shape, F32),
        in_specs=[pl.BlockSpec(memory_space=pltpu.VMEM)] * len(operands),
        out_specs=out_specs,
        scratch_shapes=scratch,
        input_output_aliases={} if first or last else {3: 0},
        cost_estimate=pl.CostEstimate(
            flops=2 * upd_rows * par_rows * par_rows, bytes_accessed=1 << 20, transcendentals=0
        ),
        compiler_params=pltpu.CompilerParams(vmem_limit_bytes=24 << 20),
    )(*operands)


def level(pivot_block, coupling_rows, trailing_block, index_map):
    child_id = lax.axis_index("front")
    pair_id = lax.axis_index("pair")
    pairs = lax.axis_size("pair")
    sibling = child_id % 4
    upd_rows = coupling_rows.shape[1]
    par_rows = PO // pairs
    parts = gather_pivot(pivot_block[0], pair_id)
    early = coupling_rows[0, :, : len(STAGES[0]) * LEAF]
    early = gather_pair(early)
    chunks, firsts = [], []

    def after_stage(index, outs):
        if index == 0:
            firsts.append(outs)
        else:
            chunks.append(gather_pair(outs[1]))

    columns = run_stages(parts, coupling_rows[0], after_stage)
    partial = partial_update(trailing_block[0], firsts[0], early, chunks[:-LATE], False)

    def local_map(which, block):
        own = lax.dynamic_slice(index_map, (which, block * upd_rows), (1, upd_rows))
        return own - block * par_rows

    maps = [
        (local_map(child_id ^ bits, pair_id), local_map(child_id ^ bits, sibling))
        for bits in range(4)
    ]
    parts = {}
    for bits in (3, 1, 2):
        (update,) = finish_update(partial, chunks[-LATE:], bits)
        parts[bits] = xor_permute(update, "front", bits)
    owned = partial_update(trailing_block[0], firsts[0], early, chunks[:-LATE], True)
    parts[0], factor = finish_update(owned, chunks[-LATE:], 0, columns)
    assembled = None
    for bits in (0, 3, 1, 2):
        assembled = extend_add(assembled, parts[bits], *maps[bits], par_rows, bits == 2)
    return (factor[None, :, :], assembled)


def solution(mesh):
    in_specs = (P("front", "pair", None), P("front", "pair", None), P("front", "pair", None), P())
    out_specs = (P("front", "pair", None), P("pair", "front", None))
    return jax.shard_map(level, mesh=mesh, in_specs=in_specs, out_specs=out_specs, check_vma=False)
```

profile of v0, /device:TPU:80, one launch (start us, length us, event | category | flops | bytes accessed | tf_op | source)
XLA Modules:
  0.0 140.8 jit_solution(6552302580277213443)
XLA Ops:
  0.6 1.0 dynamic-slice_bitcast_fusion
  1.6 3.1 %collective-permute-start.1 = (f32[192,384]{1,0:T(8,128)S(1)}, f32[192,384]{1,0:T(8,128)S(1)}, u32[]{:S(2)}, u32[]{:S(2)}) collective-permute-start(f32[192,384]{1,0:T(8,128)S(1)} %dynamic-slice_bitcast_fusion), channel_id=1, source_target_pairs={{0,2},{1,3},{2,0},{3,1},{4,6},{5,7},{6,4},{7,5},{8,10},{9,11},{10,... | collective-permute-start | bytes 884744 | tf_op jit(solution)/shard_map/ppermute | solution.py:18
  4.7 0.0 collective-permute-start
  4.8 7.2 %collective-permute-done.1.refs_2_ = f32[192,384]{1,0:T(8,128)S(1)} collective-permute-done((f32[192,384]{1,0:T(8,128)S(1)}, f32[192,384]{1,0:T(8,128)S(1)}, u32[]{:S(2)}, u32[]{:S(2)}) %collective-permute-start.1) | collective-permute-done | bytes 294944 | tf_op jit(solution)/shard_map/ppermute | solution.py:18
  12.0 0.0 collective-permute-start.2
  12.0 1.9 %slice_bitcast_fusion = f32[576,256]{1,0:T(8,128)} fusion(f32[1,576,768]{2,1,0:T(8,128)} %param.5), kind=kLoop, calls=%fused_computation | loop fusion | bytes 1179648 | tf_op jit(solution)/shard_map/squeeze | solution.py:494
  13.9 3.0 %collective-permute-start.4 = (f32[576,256]{1,0:T(8,128)}, f32[576,256]{1,0:T(8,128)S(1)}, u32[]{:S(2)}, u32[]{:S(2)}) collective-permute-start(f32[576,256]{1,0:T(8,128)} %slice_bitcast_fusion), channel_id=1, source_target_pairs={{0,2},{1,3},{2,0},{3,1},{4,6},{5,7},{6,4},{7,5},{8,10},{9,11},{10,... | collective-permute-start | bytes 1769480 | tf_op jit(solution)/shard_map/ppermute | solution.py:18
  16.9 0.2 collective-permute-start.3
  17.2 0.0 collective-permute-done.refs_1_
  17.2 7.2 %shard_map.59 = (f32[576,256]{1,0:T(8,128)S(1)}, bf16[576,256]{1,0:T(8,128)(2,1)S(1)}, bf16[576,256]{1,0:T(8,128)(2,1)S(1)}, bf16[256,768]{1,0:T(8,128)(2,1)S(1)...) custom-call(f32[192,768]{1,0:T(8,128)} %bitcast.12, ...), custom_call_target="tpu_custom_call" | custom-call | flops 4000000000 | bytes 1048576 | tf_op jit(solution)/shard_map/pallas_call | solution.py:267
  24.4 0.6 copy-done.7
  25.0 7.0 %shard_map.60 = (f32[576,256]{1,0:T(8,128)S(1)}, bf16[576,256]{1,0:T(8,128)(2,1)}, bf16[576,256]{1,0:T(8,128)(2,1)S(1)}, bf16[256,768]{1,0:T(8,128)(2,1)S(1)}, b...) custom-call(f32[768,768]{1,0:T(8,128)S(1)} %get-tuple-element.27.refs_0_, ...), custom_call_target="tpu_custom_call" | custom-call | flops 4000000000 | bytes 1048576 | tf_op jit(solution)/shard_map/pallas_call | solution.py:267
  32.1 0.9 collective-permute-start.7
  33.0 0.0 collective-permute-done.4.refs_3_
  33.0 0.0 collective-permute-start.5
  33.0 8.3 %shard_map.62 = (f32[576,256]{1,0:T(8,128)S(1)}, bf16[576,256]{1,0:T(8,128)(2,1)S(1)}, bf16[576,256]{1,0:T(8,128)(2,1)}, bf16[256,768]{1,0:T(8,128)(2,1)}, bf16[...) custom-call(f32[768,768]{1,0:T(8,128)S(1)} %get-tuple-element.27.refs_0_, ...), custom_call_target="tpu_custom_call" | custom-call | flops 4000000000 | bytes 1048576 | tf_op jit(solution)/shard_map/pallas_call | solution.py:267
  41.4 2.6 %collective-permute-start.10 = (bf16[576,256]{1,0:T(8,128)(2,1)S(1)}, bf16[576,256]{1,0:T(8,128)(2,1)S(1)}, u32[]{:S(2)}, u32[]{:S(2)}) collective-permute-start(bf16[576,256]{1,0:T(8,128)(2,1)S(1)} %get-tuple-element.38.refs_0_), channel_id=1, source_target_pairs={{0,2},{1,3},{2,0},{3,1},{4,6},{5,7},{6,4},{7,5},{8,10},{9,11},{10,... | collective-permute-start | bytes 884744 | tf_op jit(solution)/shard_map/ppermute | solution.py:18
  44.0 0.2 collective-permute-start.6
  44.1 0.0 collective-permute-done.7.refs_10_
  44.2 0.3 collective-permute-start.8
  44.5 1.1 dynamic-slice_subtract_fusion
  45.6 0.0 collective-permute-done.3.refs_2_
  45.6 0.3 collective-permute-start.9
  45.9 6.3 %collective-permute-done.10.refs_2_ = bf16[576,256]{1,0:T(8,128)(2,1)S(1)} collective-permute-done((bf16[576,256]{1,0:T(8,128)(2,1)S(1)}, bf16[576,256]{1,0:T(8,128)(2,1)S(1)}, u32[]{:S(2)}, u32[]{:S(2)}) %collective-permute-start.10) | collective-permute-done | bytes 294944 | tf_op jit(solution)/shard_map/ppermute | solution.py:18
  52.2 0.0 collective-permute-start.11
  52.2 0.0 collective-permute-done.6.refs_9_
  52.2 0.0 collective-permute-done.5.refs_4_
  52.3 0.0 copy-start
  52.3 2.5 %copy-done = f32[1,576,2304]{2,1,0:T(8,128)S(1)} copy-done((f32[1,576,2304]{2,1,0:T(8,128)S(1)}, f32[1,576,2304]{2,1,0:T(8,128)}, u32[]{:S(2)}) %copy-start) | copy-done | bytes 5308440
  54.8 1.0 copy-done.2
  55.8 1.0 copy-done.4
  56.8 1.0 copy-done.6
  57.7 0.9 copy-done.8
  58.6 9.1 %shard_map.64.w_ref = f32[4,576,576]{2,1,0:T(8,128)S(1)} custom-call(f32[576,2304]{1,0:T(8,128)S(1)} %bitcast.8, bf16[576,256]{1,0:T(8,128)(2,1)S(1)} %copy-done.6, f32[576,256]{1,0:T(8,128)S(1)} %collective-permute-done.3.refs_2_, f32[576,256]{1,0:T(8,128)S(1)} %collective-permute-done.4.refs_3_, f32[576,256]{1,0:T(8,128)} %collective-permute-done.5.refs_4_, ...), custom_call_target="tpu_custom_call" | custom-call | flops 8000000000 | bytes 1048576 | tf_op jit(solution)/shard_map/pallas_call | solution.py:361
  67.8 0.0 collective-permute-done.9.refs_1_
  67.8 0.5 shard_map.65
  68.3 0.1 collective-permute-start.12
  68.4 0.5 shard_map.66
  68.9 1.5 %collective-permute-start.13 = (bf16[576,576]{1,0:T(8,128)(2,1)S(1)}, bf16[576,576]{1,0:T(8,128)(2,1)S(1)}, u32[]{:S(2)}, u32[]{:S(2)}) collective-permute-start(bf16[576,576]{1,0:T(8,128)(2,1)S(1)} %shard_map.66), channel_id=1, source_target_pairs={{0,4},{4,0},{8,12},{12,8},{16,20},{20,16},{24,28},{28,24},{32,36},... | collective-permute-start | bytes 1990664 | tf_op jit(solution)/shard_map/ppermute | solution.py:18
  70.5 0.5 shard_map.67
  71.0 2.4 %collective-permute-start.14 = (bf16[576,576]{1,0:T(8,128)(2,1)S(1)}, bf16[576,576]{1,0:T(8,128)(2,1)S(1)}, u32[]{:S(2)}, u32[]{:S(2)}) collective-permute-start(bf16[576,576]{1,0:T(8,128)(2,1)S(1)} %shard_map.67), channel_id=1, source_target_pairs={{0,12},{4,8},{8,4},{12,0},{16,28},{20,24},{24,20},{28,16},{32,44},... | collective-permute-start | bytes 1990664 | tf_op jit(solution)/shard_map/ppermute | solution.py:18
  73.4 4.9 %shard_map.61.w_ref = f32[4,576,576]{2,1,0:T(8,128)S(1)} custom-call(f32[576,2304]{1,0:T(8,128)S(1)} %bitcast.9, bf16[576,256]{1,0:T(8,128)(2,1)S(1)} %copy-done.6, f32[576,256]{1,0:T(8,128)S(1)} %collective-permute-done.3.refs_2_, f32[576,256]{1,0:T(8,128)S(1)} %collective-permute-done.4.refs_3_, f32[576,256]{1,0:T(8,128)} %collective-permute-done.5.refs_4_, ...), custom_call_target="tpu_custom_call" | custom-call | flops 8000000000 | bytes 1048576 | tf_op jit(solution)/shard_map/pallas_call | solution.py:361
  78.2 1.6 %shard_map.63 = (bf16[576,576]{1,0:T(8,128)(2,1)S(1)}, f32[576,768]{1,0:T(8,128)}) custom-call(f32[4,576,576]{2,1,0:T(8,128)S(1)} %shard_map.61.w_ref, bf16[576,256]{1,0:T(8,128)(2,1)S(1)} %get-tuple-element.38.refs_0_, bf16[576,256]{1,0:T(8,128)(2,1)S(1)} %collective-permute-done.9.refs_1_, bf16[576,256]{1,0:T(8,128)(2,1)S(1)} %collective-permute-done.10.refs_2_, ...), custom_call_target="tpu_custom_call" | custom-call | flops 500000000 | bytes 1048576 | tf_op jit(solution)/shard_map/pallas_call | solution.py:408
  79.9 1.3 shard_map.68.refs_3_
  81.2 54.2 %collective-permute-done.14.refs_0_ = bf16[576,576]{1,0:T(8,128)(2,1)S(1)} collective-permute-done((bf16[576,576]{1,0:T(8,128)(2,1)S(1)}, bf16[576,576]{1,0:T(8,128)(2,1)S(1)}, u32[]{:S(2)}, u32[]{:S(2)}) %collective-permute-start.14) | collective-permute-done | bytes 663584 | tf_op jit(solution)/shard_map/ppermute | solution.py:18
  135.3 1.5 %shard_map.69.refs_3_ = f32[768,768]{1,0:T(8,128)S(1)} custom-call(bf16[576,576]{1,0:T(8,128)(2,1)S(1)} %collective-permute-done.14.refs_0_, s32[1,576]{1,0:T(1,128)S(1)} %get-tuple-element.46.refs_1_, s32[1,576]{1,0:T(1,128)S(1)} %get-tuple-element.45.refs_2_, f32[768,768]{1,0:T(8,128)S(1)} %shard_map.68.refs_3_), custom_call_target="tpu_custom_call", output_to_operand_aliasing={{}: (3, {})} | custom-call | flops 679477248 | bytes 1048576 | tf_op jit(solution)/shard_map/pallas_call | solution.py:472
  136.8 1.5 %shard_map.70.refs_3_ = f32[768,768]{1,0:T(8,128)S(1)} custom-call(bf16[576,576]{1,0:T(8,128)(2,1)S(1)} %collective-permute-done.13.refs_0_, s32[1,576]{1,0:T(1,128)S(1)} %get-tuple-element.48.refs_1_, s32[1,576]{1,0:T(1,128)S(1)} %get-tuple-element.47.refs_2_, f32[768,768]{1,0:T(8,128)S(1)} %shard_map.69.refs_3_), custom_call_target="tpu_custom_call", output_to_operand_aliasing={{}: (3, {})} | custom-call | flops 679477248 | bytes 1048576 | tf_op jit(solution)/shard_map/pallas_call | solution.py:472
  138.3 2.4 %shard_map.71 = f32[768,1,768]{2,1,0:T(1,128)} custom-call(bf16[576,576]{1,0:T(8,128)(2,1)S(1)} %collective-permute-done.12.refs_0_, s32[1,576]{1,0:T(1,128)S(1)} %get-tuple-element.50.refs_1_, s32[1,576]{1,0:T(1,128)S(1)} %get-tuple-element.49.refs_2_, f32[768,768]{1,0:T(8,128)S(1)} %shard_map.70.refs_3_), custom_call_target="tpu_custom_call" | custom-call | flops 679477248 | bytes 1048576 | tf_op jit(solution)/shard_map/pallas_call | solution.py:472
  (16 shorter events, 0.0 us)
Async XLA Ops:
  1.6 10.3 %collective-permute-start.1 = (f32[192,384]{1,0:T(8,128)S(1)}, f32[192,384]{1,0:T(8,128)S(1)}, u32[]{:S(2)}, u32[]{:S(2)}) collective-permute-start(f32[192,384]{1,0:T(8,128)S(1)} %dynamic-slice_bitcast_fusion), channel_id=1, source_target_pairs={{0,2},{1,3},{2,0},{3,1},{4,6},{5,7},{6,4},{7,5},{8,10},{9,11},{10,... | collective-permute-start | bytes 884744 | tf_op jit(solution)/shard_map/ppermute | solution.py:18
  4.7 12.4 %collective-permute-start = (f32[192,768]{1,0:T(8,128)}, f32[192,768]{1,0:T(8,128)S(1)}, u32[]{:S(2)}, u32[]{:S(2)}) collective-permute-start(f32[192,768]{1,0:T(8,128)} %bitcast.11), channel_id=1, source_target_pairs={{0,1},{1,0},{2,3},{3,2},{4,5},{5,4},{6,7},{7,6},{8,9},{9,8},{10,11... | collective-permute-start | bytes 1769480 | tf_op jit(solution)/shard_map/ppermute | solution.py:18
  12.0 5.2 %collective-permute-start.2 = (f32[192,384]{1,0:T(8,128)S(1)}, f32[192,384]{1,0:T(8,128)S(1)}, u32[]{:S(2)}, u32[]{:S(2)}) collective-permute-start(f32[192,384]{1,0:T(8,128)S(1)} %collective-permute-done.1.refs_2_), channel_id=1, source_target_pairs={{0,1},{1,0},{2,3},{3,2},{4,5},{5,4},{6,7},{7,6},{8,9},{9,8},{10,11... | collective-permute-start | bytes 884744 | tf_op jit(solution)/shard_map/ppermute | solution.py:18
  13.9 19.1 %collective-permute-start.4 = (f32[576,256]{1,0:T(8,128)}, f32[576,256]{1,0:T(8,128)S(1)}, u32[]{:S(2)}, u32[]{:S(2)}) collective-permute-start(f32[576,256]{1,0:T(8,128)} %slice_bitcast_fusion), channel_id=1, source_target_pairs={{0,2},{1,3},{2,0},{3,1},{4,6},{5,7},{6,4},{7,5},{8,10},{9,11},{10,... | collective-permute-start | bytes 1769480 | tf_op jit(solution)/shard_map/ppermute | solution.py:18
  16.9 28.7 %collective-permute-start.3 = (f32[576,256]{1,0:T(8,128)}, f32[576,256]{1,0:T(8,128)S(1)}, u32[]{:S(2)}, u32[]{:S(2)}) collective-permute-start(f32[576,256]{1,0:T(8,128)} %slice_bitcast_fusion), channel_id=1, source_target_pairs={{0,1},{1,0},{2,3},{3,2},{4,5},{5,4},{6,7},{7,6},{8,9},{9,8},{10,11... | collective-permute-start | bytes 1769480 | tf_op jit(solution)/shard_map/ppermute | solution.py:18
  24.4 0.7 copy-start.7
  25.0 8.0 %copy-start.1 = (bf16[256,768]{1,0:T(8,128)(2,1)}, bf16[256,768]{1,0:T(8,128)(2,1)S(1)}, u32[]{:S(2)}) copy-start(bf16[256,768]{1,0:T(8,128)(2,1)S(1)} %get-tuple-element.25.refs_4_.refs_6_) | copy-start | bytes 1179652
  25.0 8.0 %copy-start.3 = (bf16[256,768]{1,0:T(8,128)(2,1)}, bf16[256,768]{1,0:T(8,128)(2,1)S(1)}, u32[]{:S(2)}) copy-start(bf16[256,768]{1,0:T(8,128)(2,1)S(1)} %get-tuple-element.26.refs_5_.refs_7_) | copy-start | bytes 1179652
  25.0 8.0 %copy-start.5 = (bf16[576,256]{1,0:T(8,128)(2,1)}, bf16[576,256]{1,0:T(8,128)(2,1)S(1)}, u32[]{:S(2)}) copy-start(bf16[576,256]{1,0:T(8,128)(2,1)S(1)} %get-tuple-element.23.refs_2_.refs_1_) | copy-start | bytes 884740
  32.1 12.1 %collective-permute-start.7 = (bf16[576,256]{1,0:T(8,128)(2,1)}, bf16[576,256]{1,0:T(8,128)(2,1)}, u32[]{:S(2)}, u32[]{:S(2)}) collective-permute-start(bf16[576,256]{1,0:T(8,128)(2,1)} %get-tuple-element.32.refs_8_), channel_id=1, source_target_pairs={{0,2},{1,3},{2,0},{3,1},{4,6},{5,7},{6,4},{7,5},{8,10},{9,11},{10,... | collective-permute-start | bytes 884744 | tf_op jit(solution)/shard_map/ppermute | solution.py:18
  33.0 19.3 %collective-permute-start.5 = (f32[576,256]{1,0:T(8,128)S(1)}, f32[576,256]{1,0:T(8,128)}, u32[]{:S(2)}, u32[]{:S(2)}) collective-permute-start(f32[576,256]{1,0:T(8,128)S(1)} %collective-permute-done.4.refs_3_), channel_id=1, source_target_pairs={{0,1},{1,0},{2,3},{3,2},{4,5},{5,4},{6,7},{7,6},{8,9},{9,8},{10,11... | collective-permute-start | bytes 1769480 | tf_op jit(solution)/shard_map/ppermute | solution.py:18
  41.4 10.9 %collective-permute-start.10 = (bf16[576,256]{1,0:T(8,128)(2,1)S(1)}, bf16[576,256]{1,0:T(8,128)(2,1)S(1)}, u32[]{:S(2)}, u32[]{:S(2)}) collective-permute-start(bf16[576,256]{1,0:T(8,128)(2,1)S(1)} %get-tuple-element.38.refs_0_), channel_id=1, source_target_pairs={{0,2},{1,3},{2,0},{3,1},{4,6},{5,7},{6,4},{7,5},{8,10},{9,11},{10,... | collective-permute-start | bytes 884744 | tf_op jit(solution)/shard_map/ppermute | solution.py:18
  44.0 8.3 %collective-permute-start.6 = (bf16[576,256]{1,0:T(8,128)(2,1)}, bf16[576,256]{1,0:T(8,128)(2,1)}, u32[]{:S(2)}, u32[]{:S(2)}) collective-permute-start(bf16[576,256]{1,0:T(8,128)(2,1)} %get-tuple-element.32.refs_8_), channel_id=1, source_target_pairs={{0,1},{1,0},{2,3},{3,2},{4,5},{5,4},{6,7},{7,6},{8,9},{9,8},{10,11... | collective-permute-start | bytes 884744 | tf_op jit(solution)/shard_map/ppermute | solution.py:18
  44.2 8.1 %collective-permute-start.8 = (bf16[576,256]{1,0:T(8,128)(2,1)}, bf16[576,256]{1,0:T(8,128)(2,1)}, u32[]{:S(2)}, u32[]{:S(2)}) collective-permute-start(bf16[576,256]{1,0:T(8,128)(2,1)} %collective-permute-done.7.refs_10_), channel_id=1, source_target_pairs={{0,1},{1,0},{2,3},{3,2},{4,5},{5,4},{6,7},{7,6},{8,9},{9,8},{10,11... | collective-permute-start | bytes 884744 | tf_op jit(solution)/shard_map/ppermute | solution.py:18
  45.6 22.1 %collective-permute-start.9 = (bf16[576,256]{1,0:T(8,128)(2,1)S(1)}, bf16[576,256]{1,0:T(8,128)(2,1)S(1)}, u32[]{:S(2)}, u32[]{:S(2)}) collective-permute-start(bf16[576,256]{1,0:T(8,128)(2,1)S(1)} %get-tuple-element.38.refs_0_), channel_id=1, source_target_pairs={{0,1},{1,0},{2,3},{3,2},{4,5},{5,4},{6,7},{7,6},{8,9},{9,8},{10,11... | collective-permute-start | bytes 884744 | tf_op jit(solution)/shard_map/ppermute | solution.py:18
  52.2 15.6 %collective-permute-start.11 = (bf16[576,256]{1,0:T(8,128)(2,1)S(1)}, bf16[576,256]{1,0:T(8,128)(2,1)S(1)}, u32[]{:S(2)}, u32[]{:S(2)}) collective-permute-start(bf16[576,256]{1,0:T(8,128)(2,1)S(1)} %collective-permute-done.10.refs_2_), channel_id=1, source_target_pairs={{0,1},{1,0},{2,3},{3,2},{4,5},{5,4},{6,7},{7,6},{8,9},{9,8},{10,11... | collective-permute-start | bytes 884744 | tf_op jit(solution)/shard_map/ppermute | solution.py:18
  52.3 2.5 %copy-start = (f32[1,576,2304]{2,1,0:T(8,128)S(1)}, f32[1,576,2304]{2,1,0:T(8,128)}, u32[]{:S(2)}) copy-start(f32[1,576,2304]{2,1,0:T(8,128)} %param.6) | copy-start | bytes 15925252
  54.8 1.0 copy-start.2
  55.8 1.0 copy-start.4
  56.8 1.0 copy-start.6
  57.7 0.9 copy-start.8
  68.3 69.9 %collective-permute-start.12 = (bf16[576,576]{1,0:T(8,128)(2,1)S(1)}, bf16[576,576]{1,0:T(8,128)(2,1)S(1)}, u32[]{:S(2)}, u32[]{:S(2)}) collective-permute-start(bf16[576,576]{1,0:T(8,128)(2,1)S(1)} %shard_map.65), channel_id=1, source_target_pairs={{0,8},{4,12},{8,0},{12,4},{16,24},{20,28},{24,16},{28,20},{32,40},... | collective-permute-start | bytes 1990664 | tf_op jit(solution)/shard_map/ppermute | solution.py:18
  68.9 67.9 %collective-permute-start.13 = (bf16[576,576]{1,0:T(8,128)(2,1)S(1)}, bf16[576,576]{1,0:T(8,128)(2,1)S(1)}, u32[]{:S(2)}, u32[]{:S(2)}) collective-permute-start(bf16[576,576]{1,0:T(8,128)(2,1)S(1)} %shard_map.66), channel_id=1, source_target_pairs={{0,4},{4,0},{8,12},{12,8},{16,20},{20,16},{24,28},{28,24},{32,36},... | collective-permute-start | bytes 1990664 | tf_op jit(solution)/shard_map/ppermute | solution.py:18
  71.0 64.3 %collective-permute-start.14 = (bf16[576,576]{1,0:T(8,128)(2,1)S(1)}, bf16[576,576]{1,0:T(8,128)(2,1)S(1)}, u32[]{:S(2)}, u32[]{:S(2)}) collective-permute-start(bf16[576,576]{1,0:T(8,128)(2,1)S(1)} %shard_map.67), channel_id=1, source_target_pairs={{0,12},{4,8},{8,4},{12,0},{16,28},{20,24},{24,20},{28,16},{32,44},... | collective-permute-start | bytes 1990664 | tf_op jit(solution)/shard_map/ppermute | solution.py:18
where the time goes:
time: 141 us
  waiting for transfers between devices  67.7 us (48%)
  Pallas kernels  46.3 us (33%)
  starting transfers between devices  14.7 us (10%)
  local copies, waits for them, and re-layouts  9.92 us (7%)
    ppermute x15, waiting for transfers between devices, xor_permute(): lax.ppermute(value, axis, [(i, i ^ bits) for i in range(lax.axis_size(axi...  67.7 us
    pallas_call x3, Pallas kernels, stage(): pl.pallas_call(functools.partial(stage_kernel, stages, index, blocks), ou...  22.6 us
    ppermute x15, starting transfers between devices, xor_permute(): lax.ppermute(value, axis, [(i, i ^ bits) for i in range(lax.axis_size(axi...  14.7 us
    pallas_call x2, Pallas kernels, partial_update(): pl.pallas_call(functools.partial(partial_kernel, own_block), out_shape=ja...  14 us
    unnamed x18, local copies, waits for them, and re-layouts  7.01 us
    pallas_call x4, Pallas kernels, extend_add(): pl.pallas_call(functools.partial(extend_kernel, first, last), out_shape=j...  6.56 us
    pallas_call x4, Pallas kernels, finish_update(): pl.pallas_call(functools.partial(finish_kernel, bits, len(sources)), out_...  3.15 us
  transfers between devices with their start and end apart: 15, of which 3 were waited for; matrix products, arithmetic and copies ran while one was open for 2% of the time, Pallas kernels for 31%

commit v1 on v0

--- a/solution.py
+++ b/solution.py
@@ -296,6 +296,7 @@
 
 
 LATE = 1
+FIRST = 3
 
 
 def place_panels(sources, all_ref, at):
@@ -309,7 +310,7 @@
     return lax.dot_general(left, right, (((1,), (1,)), ((), ())), preferred_element_type=F32)
 
 
-def partial_kernel(own_block, *refs):
+def partial_kernel(ahead, *refs):
     t_ref, own_ref, near, far, cross, inverse_ref, u_high, u_low, *sources, w_ref, all_ref = refs
     pair_id = lax.axis_index("pair")
     width = own_ref.shape[1]
@@ -343,7 +344,7 @@
         own = jnp.concatenate(own, 1)
         for column in range(4):
 
-            @pl.when((sibling == column) == own_block)
+            @pl.when((sibling == column ^ FIRST) == ahead)
             def _():
                 trailing = t_ref[rows, column * upd_rows : (column + 1) * upd_rows]
                 w_ref[sibling ^ column, rows, :] = trailing - gram(own, all_ref[column])
@@ -353,13 +354,13 @@
     lax.fori_loop(0, 4, rows_of, 0)
 
 
-def partial_update(trailing, first, early, chunks, own_block):
+def partial_update(trailing, first, early, chunks, ahead):
     upd_rows = trailing.shape[0]
     width = first[1].shape[1] + sum(chunk[0].shape[1] for chunk in chunks)
     start = [trailing, first[1], *early[1:], first[9], first[3], first[4]]
     sources = [source for chunk in chunks for source in chunk]
     return pl.pallas_call(
-        functools.partial(partial_kernel, own_block),
+        functools.partial(partial_kernel, ahead),
         out_shape=jax.ShapeDtypeStruct((4, upd_rows, upd_rows), F32),
         in_specs=[VMEM] * (len(start) + len(sources)),
         out_specs=VMEM,
@@ -502,7 +503,8 @@
             chunks.append(gather_pair(outs[1]))
 
     columns = run_stages(parts, coupling_rows[0], after_stage)
-    partial = partial_update(trailing_block[0], firsts[0], early, chunks[:-LATE], False)
+    ahead = partial_update(trailing_block[0], firsts[0], early, chunks[:-LATE], True)
+    others = partial_update(trailing_block[0], firsts[0], early, chunks[:-LATE], False)
 
     def local_map(which, block):
         own = lax.dynamic_slice(index_map, (which, block * upd_rows), (1, upd_rows))
@@ -513,11 +515,11 @@
         for bits in range(4)
     ]
     parts = {}
-    for bits in (3, 1, 2):
+    for bits in (FIRST, 1, 2):
+        partial = ahead if bits == FIRST else others
         (update,) = finish_update(partial, chunks[-LATE:], bits)
         parts[bits] = xor_permute(update, "front", bits)
-    owned = partial_update(trailing_block[0], firsts[0], early, chunks[:-LATE], True)
-    parts[0], factor = finish_update(owned, chunks[-LATE:], 0, columns)
+    parts[0], factor = finish_update(others, chunks[-LATE:], 0, columns)
     assembled = None
     for bits in (0, 3, 1, 2):
         assembled = extend_add(assembled, parts[bits], *maps[bits], par_rows, bits == 2)

time: 141 us -> 129 us (0.915)
  the two profiles are of different devices: /device:TPU:80 before, /device:TPU:1 now
where the time goes in v1:
time: 129 us
  waiting for transfers between devices  51.4 us (40%)
  Pallas kernels  44.7 us (35%)
  starting transfers between devices  19.5 us (15%)
  local copies, waits for them, and re-layouts  11.1 us (9%)
    ppermute x15, waiting for transfers between devices, xor_permute(): lax.ppermute(value, axis, [(i, i ^ bits) for i in range(lax.axis_size(axi...  51.4 us
    pallas_call x3, Pallas kernels, stage(): pl.pallas_call(functools.partial(stage_kernel, stages, index, blocks), ou...  20.8 us
    ppermute x15, starting transfers between devices, xor_permute(): lax.ppermute(value, axis, [(i, i ^ bits) for i in range(lax.axis_size(axi...  19.5 us
    pallas_call x2, Pallas kernels, partial_update(): pl.pallas_call(functools.partial(partial_kernel, ahead), out_shape=jax.Sh...  11.2 us
    unnamed x20, local copies, waits for them, and re-layouts  8.99 us
    pallas_call x4, Pallas kernels, extend_add(): pl.pallas_call(functools.partial(extend_kernel, first, last), out_shape=j...  6.54 us
    pallas_call x4, Pallas kernels, finish_update(): pl.pallas_call(functools.partial(finish_kernel, bits, len(sources)), out_...  6.09 us
  transfers between devices with their start and end apart: 15, of which 4 were waited for; matrix products, arithmetic and copies ran while one was open for 2% of the time, Pallas kernels for 32%

profile of v1, /device:TPU:1, one launch (start us, length us, event | category | flops | bytes accessed | tf_op | source)
XLA Modules:
  0.0 128.8 jit_solution(14242659723832782812)
XLA Ops:
  0.6 1.0 dynamic-slice_bitcast_fusion
  1.6 3.6 %collective-permute-start.1 = (f32[192,384]{1,0:T(8,128)S(1)}, f32[192,384]{1,0:T(8,128)S(1)}, u32[]{:S(2)}, u32[]{:S(2)}) collective-permute-start(f32[192,384]{1,0:T(8,128)S(1)} %dynamic-slice_bitcast_fusion), channel_id=1, source_target_pairs={{0,2},{1,3},{2,0},{3,1},{4,6},{5,7},{6,4},{7,5},{8,10},{9,11},{10,... | collective-permute-start | bytes 884744 | tf_op jit(solution)/shard_map/ppermute | solution.py:18
  5.3 1.0 collective-permute-start
  6.2 4.7 %collective-permute-done.1.refs_2_ = f32[192,384]{1,0:T(8,128)S(1)} collective-permute-done((f32[192,384]{1,0:T(8,128)S(1)}, f32[192,384]{1,0:T(8,128)S(1)}, u32[]{:S(2)}, u32[]{:S(2)}) %collective-permute-start.1) | collective-permute-done | bytes 294944 | tf_op jit(solution)/shard_map/ppermute | solution.py:18
  11.0 2.3 %collective-permute-start.2 = (f32[192,384]{1,0:T(8,128)S(1)}, f32[192,384]{1,0:T(8,128)S(1)}, u32[]{:S(2)}, u32[]{:S(2)}) collective-permute-start(f32[192,384]{1,0:T(8,128)S(1)} %collective-permute-done.1.refs_2_), channel_id=1, source_target_pairs={{0,1},{1,0},{2,3},{3,2},{4,5},{5,4},{6,7},{7,6},{8,9},{9,8},{10,11... | collective-permute-start | bytes 884744 | tf_op jit(solution)/shard_map/ppermute | solution.py:18
  13.3 1.1 slice_bitcast_fusion
  14.4 3.1 %collective-permute-start.4 = (f32[576,256]{1,0:T(8,128)S(1)}, f32[576,256]{1,0:T(8,128)S(1)}, u32[]{:S(2)}, u32[]{:S(2)}) collective-permute-start(f32[576,256]{1,0:T(8,128)S(1)} %slice_bitcast_fusion), channel_id=1, source_target_pairs={{0,2},{1,3},{2,0},{3,1},{4,6},{5,7},{6,4},{7,5},{8,10},{9,11},{10,... | collective-permute-start | bytes 1769480 | tf_op jit(solution)/shard_map/ppermute | solution.py:18
  17.4 0.3 collective-permute-start.3
  17.7 0.0 collective-permute-done.2.refs_3_
  17.7 0.0 collective-permute-done.refs_1_
  17.7 7.2 %shard_map.59 = (f32[576,256]{1,0:T(8,128)S(1)}, bf16[576,256]{1,0:T(8,128)(2,1)S(1)}, bf16[576,256]{1,0:T(8,128)(2,1)S(1)}, bf16[256,768]{1,0:T(8,128)(2,1)S(1)...) custom-call(f32[192,768]{1,0:T(8,128)} %bitcast.14, ...), custom_call_target="tpu_custom_call" | custom-call | flops 4000000000 | bytes 1048576 | tf_op jit(solution)/shard_map/pallas_call | solution.py:267
  24.9 0.0 copy-start.2
  24.9 0.8 copy-done.2
  25.7 6.3 %shard_map.60 = (f32[576,256]{1,0:T(8,128)S(1)}, bf16[576,256]{1,0:T(8,128)(2,1)S(1)}, bf16[576,256]{1,0:T(8,128)(2,1)S(1)}, bf16[256,768]{1,0:T(8,128)(2,1)S(1)...) custom-call(f32[768,768]{1,0:T(8,128)S(1)} %get-tuple-element.27.refs_0_, ...), custom_call_target="tpu_custom_call" | custom-call | flops 4000000000 | bytes 1048576 | tf_op jit(solution)/shard_map/pallas_call | solution.py:267
  32.1 0.9 copy-done.4
  32.9 0.4 collective-permute-start.7
  33.3 0.0 collective-permute-done.4.refs_3_
  33.3 0.6 collective-permute-start.5
  33.9 7.3 %shard_map.62 = (f32[576,256]{1,0:T(8,128)S(1)}, bf16[576,256]{1,0:T(8,128)(2,1)S(1)}, bf16[576,256]{1,0:T(8,128)(2,1)}, bf16[256,768]{1,0:T(8,128)(2,1)}, bf16[...) custom-call(f32[768,768]{1,0:T(8,128)S(1)} %get-tuple-element.27.refs_0_, ...), custom_call_target="tpu_custom_call" | custom-call | flops 4000000000 | bytes 1048576 | tf_op jit(solution)/shard_map/pallas_call | solution.py:267
  41.3 0.9 copy-done.6
  42.1 2.5 %collective-permute-start.10 = (bf16[576,256]{1,0:T(8,128)(2,1)S(1)}, bf16[576,256]{1,0:T(8,128)(2,1)S(1)}, u32[]{:S(2)}, u32[]{:S(2)}) collective-permute-start(bf16[576,256]{1,0:T(8,128)(2,1)S(1)} %get-tuple-element.38.refs_0_), channel_id=1, source_target_pairs={{0,2},{1,3},{2,0},{3,1},{4,6},{5,7},{6,4},{7,5},{8,10},{9,11},{10,... | collective-permute-start | bytes 884744 | tf_op jit(solution)/shard_map/ppermute | solution.py:18
  44.6 0.3 collective-permute-start.6
  44.9 0.0 collective-permute-done.7.refs_10_
  44.9 0.2 collective-permute-start.8
  45.1 0.3 collective-permute-start.9
  45.4 6.8 %collective-permute-done.10.refs_2_ = bf16[576,256]{1,0:T(8,128)(2,1)S(1)} collective-permute-done((bf16[576,256]{1,0:T(8,128)(2,1)S(1)}, bf16[576,256]{1,0:T(8,128)(2,1)S(1)}, u32[]{:S(2)}, u32[]{:S(2)}) %collective-permute-start.10) | collective-permute-done | bytes 294944 | tf_op jit(solution)/shard_map/ppermute | solution.py:18
  52.2 0.9 collective-permute-start.11
  53.1 4.2 %shard_map.66.w_ref = f32[4,576,576]{2,1,0:T(8,128)S(1)} custom-call(f32[576,2304]{1,0:T(8,128)S(1)} %bitcast.10, bf16[576,256]{1,0:T(8,128)(2,1)S(1)} %get-tuple-element.23.refs_2_.refs_1_, f32[576,256]{1,0:T(8,128)S(1)} %collective-permute-done.3.refs_2_, f32[576,256]{1,0:T(8,128)S(1)} %collective-permute-done.4.refs_3_, ...), custom_call_target="tpu_custom_call" | custom-call | flops 8000000000 | bytes 1048576 | tf_op jit(solution)/shard_map/pallas_call | solution.py:362
  57.3 1.4 %shard_map.67 = bf16[576,576]{1,0:T(8,128)(2,1)} custom-call(f32[4,576,576]{2,1,0:T(8,128)S(1)} %shard_map.66.w_ref, bf16[576,256]{1,0:T(8,128)(2,1)S(1)} %get-tuple-element.38.refs_0_, bf16[576,256]{1,0:T(8,128)(2,1)S(1)} %collective-permute-done.9.refs_1_, bf16[576,256]{1,0:T(8,128)(2,1)S(1)} %collective-permute-done.10.refs_2_, ...), custom_call_target="tpu_custom_call" | custom-call | flops 500000000 | bytes 1048576 | tf_op jit(solution)/shard_map/pallas_call | solution.py:409
  58.7 3.7 %collective-permute-start.14 = (bf16[576,576]{1,0:T(8,128)(2,1)}, bf16[576,576]{1,0:T(8,128)(2,1)S(1)}, u32[]{:S(2)}, u32[]{:S(2)}) collective-permute-start(bf16[576,576]{1,0:T(8,128)(2,1)} %shard_map.67), channel_id=1, source_target_pairs={{0,12},{4,8},{8,4},{12,0},{16,28},{20,24},{24,20},{28,16},{32,44},... | collective-permute-start | bytes 1990664 | tf_op jit(solution)/shard_map/ppermute | solution.py:18
  62.4 7.0 %shard_map.61.w_ref = f32[4,576,576]{2,1,0:T(8,128)S(1)} custom-call(f32[576,2304]{1,0:T(8,128)S(1)} %bitcast.11, bf16[576,256]{1,0:T(8,128)(2,1)S(1)} %get-tuple-element.23.refs_2_.refs_1_, f32[576,256]{1,0:T(8,128)S(1)} %collective-permute-done.3.refs_2_, f32[576,256]{1,0:T(8,128)S(1)} %collective-permute-done.4.refs_3_, ...), custom_call_target="tpu_custom_call" | custom-call | flops 8000000000 | bytes 1048576 | tf_op jit(solution)/shard_map/pallas_call | solution.py:362
  69.5 1.7 %shard_map.65 = bf16[576,576]{1,0:T(8,128)(2,1)} custom-call(f32[4,576,576]{2,1,0:T(8,128)S(1)} %shard_map.61.w_ref, bf16[576,256]{1,0:T(8,128)(2,1)S(1)} %get-tuple-element.38.refs_0_, bf16[576,256]{1,0:T(8,128)(2,1)S(1)} %collective-permute-done.9.refs_1_, bf16[576,256]{1,0:T(8,128)(2,1)S(1)} %collective-permute-done.10.refs_2_, ...), custom_call_target="tpu_custom_call" | custom-call | flops 500000000 | bytes 1048576 | tf_op jit(solution)/shard_map/pallas_call | solution.py:409
  71.2 0.4 collective-permute-start.13
  71.6 0.6 copy-done
  72.2 1.4 %shard_map.64 = bf16[576,576]{1,0:T(8,128)(2,1)} custom-call(f32[4,576,576]{2,1,0:T(8,128)S(1)} %shard_map.61.w_ref, bf16[576,256]{1,0:T(8,128)(2,1)S(1)} %get-tuple-element.38.refs_0_, bf16[576,256]{1,0:T(8,128)(2,1)S(1)} %collective-permute-done.9.refs_1_, bf16[576,256]{1,0:T(8,128)(2,1)S(1)} %collective-permute-done.10.refs_2_, ...), custom_call_target="tpu_custom_call" | custom-call | flops 500000000 | bytes 1048576 | tf_op jit(solution)/shard_map/pallas_call | solution.py:409
  73.5 0.0 collective-permute-start.12
  73.6 1.2 dynamic-slice_subtract_fusion
  74.8 2.7 %copy-done.1 = f32[4,576,576]{2,1,0:T(8,128)S(1)} copy-done((f32[4,576,576]{2,1,0:T(8,128)S(1)}, f32[4,576,576]{2,1,0:T(8,128)}, u32[]{:S(2)}) %copy-start.1) | copy-done | bytes 5308440
  77.4 1.1 copy-done.3
  78.5 1.1 copy-done.5
  79.6 1.1 copy-done.7
  80.6 1.6 %shard_map.63 = (bf16[576,576]{1,0:T(8,128)(2,1)S(1)}, f32[576,768]{1,0:T(8,128)}) custom-call(f32[4,576,576]{2,1,0:T(8,128)S(1)} %copy-done.1, bf16[576,256]{1,0:T(8,128)(2,1)S(1)} %get-tuple-element.38.refs_0_, bf16[576,256]{1,0:T(8,128)(2,1)S(1)} %collective-permute-done.9.refs_1_, bf16[576,256]{1,0:T(8,128)(2,1)S(1)} %collective-permute-done.10.refs_2_, ...), custom_call_target="tpu_custom_call" | custom-call | flops 500000000 | bytes 1048576 | tf_op jit(solution)/shard_map/pallas_call | solution.py:409
  82.2 1.3 %shard_map.68.refs_3_ = f32[768,768]{1,0:T(8,128)S(1)} custom-call(bf16[576,576]{1,0:T(8,128)(2,1)S(1)} %get-tuple-element.43.refs_0_, s32[1,576]{1,0:T(1,128)S(1)} %get-tuple-element.51.refs_1_, s32[1,576]{1,0:T(1,128)S(1)} %get-tuple-element.44.refs_2_), custom_call_target="tpu_custom_call" | custom-call | flops 679477248 | bytes 1048576 | tf_op jit(solution)/shard_map/pallas_call | solution.py:473
  83.6 1.4 %shard_map.69.refs_3_ = f32[768,768]{1,0:T(8,128)S(1)} custom-call(bf16[576,576]{1,0:T(8,128)(2,1)S(1)} %collective-permute-done.14.refs_0_, s32[1,576]{1,0:T(1,128)S(1)} %get-tuple-element.46.refs_1_, s32[1,576]{1,0:T(1,128)S(1)} %get-tuple-element.45.refs_2_, f32[768,768]{1,0:T(8,128)S(1)} %shard_map.68.refs_3_), custom_call_target="tpu_custom_call", output_to_operand_aliasing={{}: (3, {})} | custom-call | flops 679477248 | bytes 1048576 | tf_op jit(solution)/shard_map/pallas_call | solution.py:473
  85.0 11.3 %collective-permute-done.13.refs_0_ = bf16[576,576]{1,0:T(8,128)(2,1)S(1)} collective-permute-done((bf16[576,576]{1,0:T(8,128)(2,1)}, bf16[576,576]{1,0:T(8,128)(2,1)S(1)}, u32[]{:S(2)}, u32[]{:S(2)}) %collective-permute-start.13) | collective-permute-done | bytes 663584 | tf_op jit(solution)/shard_map/ppermute | solution.py:18
  96.3 1.5 %shard_map.70.refs_3_ = f32[768,768]{1,0:T(8,128)S(1)} custom-call(bf16[576,576]{1,0:T(8,128)(2,1)S(1)} %collective-permute-done.13.refs_0_, s32[1,576]{1,0:T(1,128)S(1)} %get-tuple-element.48.refs_1_, s32[1,576]{1,0:T(1,128)S(1)} %get-tuple-element.47.refs_2_, f32[768,768]{1,0:T(8,128)S(1)} %shard_map.69.refs_3_), custom_call_target="tpu_custom_call", output_to_operand_aliasing={{}: (3, {})} | custom-call | flops 679477248 | bytes 1048576 | tf_op jit(solution)/shard_map/pallas_call | solution.py:473
  97.8 28.5 %collective-permute-done.12.refs_0_ = bf16[576,576]{1,0:T(8,128)(2,1)S(1)} collective-permute-done((bf16[576,576]{1,0:T(8,128)(2,1)}, bf16[576,576]{1,0:T(8,128)(2,1)S(1)}, u32[]{:S(2)}, u32[]{:S(2)}) %collective-permute-start.12) | collective-permute-done | bytes 663584 | tf_op jit(solution)/shard_map/ppermute | solution.py:18
  126.3 2.3 %shard_map.71 = f32[768,1,768]{2,1,0:T(1,128)} custom-call(bf16[576,576]{1,0:T(8,128)(2,1)S(1)} %collective-permute-done.12.refs_0_, s32[1,576]{1,0:T(1,128)S(1)} %get-tuple-element.50.refs_1_, s32[1,576]{1,0:T(1,128)S(1)} %get-tuple-element.49.refs_2_, f32[768,768]{1,0:T(8,128)S(1)} %shard_map.70.refs_3_), custom_call_target="tpu_custom_call" | custom-call | flops 679477248 | bytes 1048576 | tf_op jit(solution)/shard_map/pallas_call | solution.py:473
  (19 shorter events, 0.0 us)
Async XLA Ops:
  1.6 9.3 %collective-permute-start.1 = (f32[192,384]{1,0:T(8,128)S(1)}, f32[192,384]{1,0:T(8,128)S(1)}, u32[]{:S(2)}, u32[]{:S(2)}) collective-permute-start(f32[192,384]{1,0:T(8,128)S(1)} %dynamic-slice_bitcast_fusion), channel_id=1, source_target_pairs={{0,2},{1,3},{2,0},{3,1},{4,6},{5,7},{6,4},{7,5},{8,10},{9,11},{10,... | collective-permute-start | bytes 884744 | tf_op jit(solution)/shard_map/ppermute | solution.py:18
  5.3 12.4 %collective-permute-start = (f32[192,768]{1,0:T(8,128)}, f32[192,768]{1,0:T(8,128)S(1)}, u32[]{:S(2)}, u32[]{:S(2)}) collective-permute-start(f32[192,768]{1,0:T(8,128)} %bitcast.13), channel_id=1, source_target_pairs={{0,1},{1,0},{2,3},{3,2},{4,5},{5,4},{6,7},{7,6},{8,9},{9,8},{10,11... | collective-permute-start | bytes 1769480 | tf_op jit(solution)/shard_map/ppermute | solution.py:18
  11.0 6.7 %collective-permute-start.2 = (f32[192,384]{1,0:T(8,128)S(1)}, f32[192,384]{1,0:T(8,128)S(1)}, u32[]{:S(2)}, u32[]{:S(2)}) collective-permute-start(f32[192,384]{1,0:T(8,128)S(1)} %collective-permute-done.1.refs_2_), channel_id=1, source_target_pairs={{0,1},{1,0},{2,3},{3,2},{4,5},{5,4},{6,7},{7,6},{8,9},{9,8},{10,11... | collective-permute-start | bytes 884744 | tf_op jit(solution)/shard_map/ppermute | solution.py:18
  14.4 19.0 %collective-permute-start.4 = (f32[576,256]{1,0:T(8,128)S(1)}, f32[576,256]{1,0:T(8,128)S(1)}, u32[]{:S(2)}, u32[]{:S(2)}) collective-permute-start(f32[576,256]{1,0:T(8,128)S(1)} %slice_bitcast_fusion), channel_id=1, source_target_pairs={{0,2},{1,3},{2,0},{3,1},{4,6},{5,7},{6,4},{7,5},{8,10},{9,11},{10,... | collective-permute-start | bytes 1769480 | tf_op jit(solution)/shard_map/ppermute | solution.py:18
  17.4 27.7 %collective-permute-start.3 = (f32[576,256]{1,0:T(8,128)S(1)}, f32[576,256]{1,0:T(8,128)S(1)}, u32[]{:S(2)}, u32[]{:S(2)}) collective-permute-start(f32[576,256]{1,0:T(8,128)S(1)} %slice_bitcast_fusion), channel_id=1, source_target_pairs={{0,1},{1,0},{2,3},{3,2},{4,5},{5,4},{6,7},{7,6},{8,9},{9,8},{10,11... | collective-permute-start | bytes 1769480 | tf_op jit(solution)/shard_map/ppermute | solution.py:18
  24.9 0.8 copy-start.2
  25.7 27.4 %slice-start = ((s8[5308416]{0:T(1024)(128)(4,1)}), s8[4194304]{0:T(1024)(128)(4,1)S(1)}, s32[]{:S(2)}) async-start(s8[5308416]{0:T(1024)(128)(4,1)} %bitcast.8), calls=%async_computation | async-start | bytes 8388608
  32.1 0.9 copy-start.4
  32.9 12.0 %collective-permute-start.7 = (bf16[576,256]{1,0:T(8,128)(2,1)S(1)}, bf16[576,256]{1,0:T(8,128)(2,1)S(1)}, u32[]{:S(2)}, u32[]{:S(2)}) collective-permute-start(bf16[576,256]{1,0:T(8,128)(2,1)S(1)} %get-tuple-element.32.refs_8_), channel_id=1, source_target_pairs={{0,2},{1,3},{2,0},{3,1},{4,6},{5,7},{6,4},{7,5},{8,10},{9,11},{10,... | collective-permute-start | bytes 884744 | tf_op jit(solution)/shard_map/ppermute | solution.py:18
  33.3 19.7 %collective-permute-start.5 = (f32[576,256]{1,0:T(8,128)S(1)}, f32[576,256]{1,0:T(8,128)S(1)}, u32[]{:S(2)}, u32[]{:S(2)}) collective-permute-start(f32[576,256]{1,0:T(8,128)S(1)} %collective-permute-done.4.refs_3_), channel_id=1, source_target_pairs={{0,1},{1,0},{2,3},{3,2},{4,5},{5,4},{6,7},{7,6},{8,9},{9,8},{10,11... | collective-permute-start | bytes 1769480 | tf_op jit(solution)/shard_map/ppermute | solution.py:18
  33.9 19.2 %slice-start.1 = ((s8[5308416]{0:T(1024)(128)(4,1)}), s8[1114112]{0:T(1024)(128)(4,1)S(1)}, s32[]{:S(2)}) async-start(s8[5308416]{0:T(1024)(128)(4,1)} %bitcast.8), calls=%async_computation.1 | async-start | bytes 2228224
  41.3 0.9 copy-start.6
  42.1 10.1 %collective-permute-start.10 = (bf16[576,256]{1,0:T(8,128)(2,1)S(1)}, bf16[576,256]{1,0:T(8,128)(2,1)S(1)}, u32[]{:S(2)}, u32[]{:S(2)}) collective-permute-start(bf16[576,256]{1,0:T(8,128)(2,1)S(1)} %get-tuple-element.38.refs_0_), channel_id=1, source_target_pairs={{0,2},{1,3},{2,0},{3,1},{4,6},{5,7},{6,4},{7,5},{8,10},{9,11},{10,... | collective-permute-start | bytes 884744 | tf_op jit(solution)/shard_map/ppermute | solution.py:18
  44.6 8.5 %collective-permute-start.6 = (bf16[576,256]{1,0:T(8,128)(2,1)S(1)}, bf16[576,256]{1,0:T(8,128)(2,1)S(1)}, u32[]{:S(2)}, u32[]{:S(2)}) collective-permute-start(bf16[576,256]{1,0:T(8,128)(2,1)S(1)} %get-tuple-element.32.refs_8_), channel_id=1, source_target_pairs={{0,1},{1,0},{2,3},{3,2},{4,5},{5,4},{6,7},{7,6},{8,9},{9,8},{10,11... | collective-permute-start | bytes 884744 | tf_op jit(solution)/shard_map/ppermute | solution.py:18
  44.9 8.2 %collective-permute-start.8 = (bf16[576,256]{1,0:T(8,128)(2,1)S(1)}, bf16[576,256]{1,0:T(8,128)(2,1)S(1)}, u32[]{:S(2)}, u32[]{:S(2)}) collective-permute-start(bf16[576,256]{1,0:T(8,128)(2,1)S(1)} %collective-permute-done.7.refs_10_), channel_id=1, source_target_pairs={{0,1},{1,0},{2,3},{3,2},{4,5},{5,4},{6,7},{7,6},{8,9},{9,8},{10,11... | collective-permute-start | bytes 884744 | tf_op jit(solution)/shard_map/ppermute | solution.py:18
  45.1 12.2 %collective-permute-start.9 = (bf16[576,256]{1,0:T(8,128)(2,1)S(1)}, bf16[576,256]{1,0:T(8,128)(2,1)S(1)}, u32[]{:S(2)}, u32[]{:S(2)}) collective-permute-start(bf16[576,256]{1,0:T(8,128)(2,1)S(1)} %get-tuple-element.38.refs_0_), channel_id=1, source_target_pairs={{0,1},{1,0},{2,3},{3,2},{4,5},{5,4},{6,7},{7,6},{8,9},{9,8},{10,11... | collective-permute-start | bytes 884744 | tf_op jit(solution)/shard_map/ppermute | solution.py:18
  52.2 5.1 %collective-permute-start.11 = (bf16[576,256]{1,0:T(8,128)(2,1)S(1)}, bf16[576,256]{1,0:T(8,128)(2,1)S(1)}, u32[]{:S(2)}, u32[]{:S(2)}) collective-permute-start(bf16[576,256]{1,0:T(8,128)(2,1)S(1)} %collective-permute-done.10.refs_2_), channel_id=1, source_target_pairs={{0,1},{1,0},{2,3},{3,2},{4,5},{5,4},{6,7},{7,6},{8,9},{9,8},{10,11... | collective-permute-start | bytes 884744 | tf_op jit(solution)/shard_map/ppermute | solution.py:18
  58.7 24.9 %collective-permute-start.14 = (bf16[576,576]{1,0:T(8,128)(2,1)}, bf16[576,576]{1,0:T(8,128)(2,1)S(1)}, u32[]{:S(2)}, u32[]{:S(2)}) collective-permute-start(bf16[576,576]{1,0:T(8,128)(2,1)} %shard_map.67), channel_id=1, source_target_pairs={{0,12},{4,8},{8,4},{12,0},{16,28},{20,24},{24,20},{28,16},{32,44},... | collective-permute-start | bytes 1990664 | tf_op jit(solution)/shard_map/ppermute | solution.py:18
  69.4 2.7 %copy-start = (f32[4,576,576]{2,1,0:T(8,128)}, f32[4,576,576]{2,1,0:T(8,128)S(1)}, u32[]{:S(2)}) copy-start(f32[4,576,576]{2,1,0:T(8,128)S(1)} %shard_map.61.w_ref) | copy-start | bytes 15925252
  71.2 25.1 %collective-permute-start.13 = (bf16[576,576]{1,0:T(8,128)(2,1)}, bf16[576,576]{1,0:T(8,128)(2,1)S(1)}, u32[]{:S(2)}, u32[]{:S(2)}) collective-permute-start(bf16[576,576]{1,0:T(8,128)(2,1)} %shard_map.65), channel_id=1, source_target_pairs={{0,4},{4,0},{8,12},{12,8},{16,20},{20,16},{24,28},{28,24},{32,36},... | collective-permute-start | bytes 1990664 | tf_op jit(solution)/shard_map/ppermute | solution.py:18
  73.5 52.8 %collective-permute-start.12 = (bf16[576,576]{1,0:T(8,128)(2,1)}, bf16[576,576]{1,0:T(8,128)(2,1)S(1)}, u32[]{:S(2)}, u32[]{:S(2)}) collective-permute-start(bf16[576,576]{1,0:T(8,128)(2,1)} %shard_map.64), channel_id=1, source_target_pairs={{0,8},{4,12},{8,0},{12,4},{16,24},{20,28},{24,16},{28,20},{32,40},... | collective-permute-start | bytes 1990664 | tf_op jit(solution)/shard_map/ppermute | solution.py:18
  74.8 2.7 %copy-start.1 = (f32[4,576,576]{2,1,0:T(8,128)S(1)}, f32[4,576,576]{2,1,0:T(8,128)}, u32[]{:S(2)}) copy-start(f32[4,576,576]{2,1,0:T(8,128)} %copy-done) | copy-start | bytes 15925252
  77.4 1.1 copy-start.3
  78.5 1.1 copy-start.5
  79.6 1.1 copy-start.7

commit v2 on v1

--- a/solution.py
+++ b/solution.py
@@ -292,10 +292,10 @@
     return columns
 
 
-STAGES = ((0, 1), (2, 3), (4, 5))
-
-
-LATE = 1
+STAGES = ((0, 1, 2), (3, 4), (5,))
+
+
+LATE = 2
 FIRST = 3
 
 
@@ -315,11 +315,17 @@
     pair_id = lax.axis_index("pair")
     width = own_ref.shape[1]
     all_ref[pair_id, :, :width] = own_ref[...]
-    first, second = inverse_ref[0].T, inverse_ref[1].T
-    at = span(0, 1), span(1, 2)
-    corner = three(halves(three(halves(first), (u_high[at], u_low[at]))), halves(second))
-    whole = jnp.concatenate([first, -corner], 1), jnp.concatenate([0.0 * second, second], 1)
-    whole = halves(jnp.concatenate(whole, 0))
+    leaves = width // LEAF
+    solved = [[jnp.zeros((LEAF, LEAF), F32)] * leaves for _ in range(leaves)]
+    for k in range(leaves):
+        solved[k][k] = inverse_ref[k].T
+        for j in range(k):
+            total = 0.0
+            for i in range(j, k):
+                at = span(i, i + 1), span(k, k + 1)
+                total = total + three(halves(solved[j][i]), (u_high[at], u_low[at]))
+            solved[j][k] = -three(halves(total), halves(solved[k][k]))
+    whole = halves(jnp.concatenate([jnp.concatenate(row, 1) for row in solved], 0))
     tile = own_ref.shape[0] // 4
 
     def panel_rows(i, _):

time: 129 us -> 147 us (1.14)
  waiting for transfers between devices: 51.4 us -> 63.4 us
  Pallas kernels: 44.7 us -> 51.8 us
  local copies, waits for them, and re-layouts: 11.1 us -> 9.53 us
    ppermute x15, waiting for transfers between devices: 51.4 us -> 63.4 us  [xor_permute(): lax.ppermute(value, axis, [(i, i ^ bits) for i in range(lax.axis_size(axi...]
    pallas_call x2, Pallas kernels: 11.2 us -> 15 us  [partial_update(): pl.pallas_call(functools.partial(partial_kernel, ahead), out_shape=jax.Sh...]
    unnamed x20 -> x18, local copies, waits for them, and re-layouts: 8.99 us -> 6.35 us
    pallas_call x4, Pallas kernels: 6.54 us -> 8.81 us  [extend_add(): pl.pallas_call(functools.partial(extend_kernel, first, last), out_shape=j...]
  transfers between devices with their start and end apart: 15 -> 15, of which waited for: 4 -> 5; matrix products, arithmetic and copies ran while one was open for 2% -> 1% of each run, Pallas kernels for 32% -> 32%
where the time goes in v2:
time: 147 us
  waiting for transfers between devices  63.4 us (43%)
  Pallas kernels  51.8 us (35%)
  starting transfers between devices  20.2 us (14%)
  local copies, waits for them, and re-layouts  9.53 us (6%)
    ppermute x15, waiting for transfers between devices, xor_permute(): lax.ppermute(value, axis, [(i, i ^ bits) for i in range(lax.axis_size(axi...  63.4 us
    pallas_call x3, Pallas kernels, stage(): pl.pallas_call(functools.partial(stage_kernel, stages, index, blocks), ou...  21.1 us
    ppermute x15, starting transfers between devices, xor_permute(): lax.ppermute(value, axis, [(i, i ^ bits) for i in range(lax.axis_size(axi...  20.2 us
    pallas_call x2, Pallas kernels, partial_update(): pl.pallas_call(functools.partial(partial_kernel, ahead), out_shape=jax.Sh...  15 us
    pallas_call x4, Pallas kernels, extend_add(): pl.pallas_call(functools.partial(extend_kernel, first, last), out_shape=j...  8.81 us
    pallas_call x4, Pallas kernels, finish_update(): pl.pallas_call(functools.partial(finish_kernel, bits, len(sources)), out_...  6.9 us
    unnamed x18, local copies, waits for them, and re-layouts  6.35 us
  transfers between devices with their start and end apart: 15, of which 5 were waited for; matrix products, arithmetic and copies ran while one was open for 1% of the time, Pallas kernels for 32%

profile of v2, /device:TPU:1, one launch (start us, length us, event | category | flops | bytes accessed | tf_op | source)
XLA Modules:
  0.0 147.0 jit_solution(6916562604670780225)
XLA Ops:
  0.6 0.0 copy-start.6
  0.6 2.2 %slice_bitcast_fusion = f32[576,384]{1,0:T(8,128)} fusion(f32[1,576,768]{2,1,0:T(8,128)} %param.5), kind=kLoop, calls=%fused_computation | loop fusion | bytes 1769472 | tf_op jit(solution)/shard_map/squeeze | solution.py:501
  2.8 3.6 %collective-permute-start.4 = (f32[576,384]{1,0:T(8,128)}, f32[576,384]{1,0:T(8,128)S(1)}, u32[]{:S(2)}, u32[]{:S(2)}) collective-permute-start(f32[576,384]{1,0:T(8,128)} %slice_bitcast_fusion), channel_id=1, source_target_pairs={{0,2},{1,3},{2,0},{3,1},{4,6},{5,7},{6,4},{7,5},{8,10},{9,11},{10,... | collective-permute-start | bytes 2654216 | tf_op jit(solution)/shard_map/ppermute | solution.py:18
  6.4 1.0 dynamic-slice_bitcast_fusion
  7.4 0.1 collective-permute-start.1
  7.5 3.1 %collective-permute-start = (f32[192,768]{1,0:T(8,128)S(1)}, f32[192,768]{1,0:T(8,128)S(1)}, u32[]{:S(2)}, u32[]{:S(2)}) collective-permute-start(f32[192,768]{1,0:T(8,128)S(1)} %bitcast.14), channel_id=1, source_target_pairs={{0,1},{1,0},{2,3},{3,2},{4,5},{5,4},{6,7},{7,6},{8,9},{9,8},{10,11... | collective-permute-start | bytes 1769480 | tf_op jit(solution)/shard_map/ppermute | solution.py:18
  10.6 20.6 %collective-permute-done.1.refs_2_ = f32[192,384]{1,0:T(8,128)S(1)} collective-permute-done((f32[192,384]{1,0:T(8,128)S(1)}, f32[192,384]{1,0:T(8,128)S(1)}, u32[]{:S(2)}, u32[]{:S(2)}) %collective-permute-start.1) | collective-permute-done | bytes 294944 | tf_op jit(solution)/shard_map/ppermute | solution.py:18
  31.3 2.3 %collective-permute-start.2 = (f32[192,384]{1,0:T(8,128)S(1)}, f32[192,384]{1,0:T(8,128)S(1)}, u32[]{:S(2)}, u32[]{:S(2)}) collective-permute-start(f32[192,384]{1,0:T(8,128)S(1)} %collective-permute-done.1.refs_2_), channel_id=1, source_target_pairs={{0,1},{1,0},{2,3},{3,2},{4,5},{5,4},{6,7},{7,6},{8,9},{9,8},{10,11... | collective-permute-start | bytes 884744 | tf_op jit(solution)/shard_map/ppermute | solution.py:18
  33.5 0.0 collective-permute-start.3
  33.5 0.0 collective-permute-done.4.refs_3_
  33.5 0.5 collective-permute-start.5
  34.0 0.7 collective-permute-done.2.refs_3_
  34.7 10.6 %shard_map.59 = (f32[576,384]{1,0:T(8,128)S(1)}, bf16[576,384]{1,0:T(8,128)(2,1)S(1)}, bf16[576,384]{1,0:T(8,128)(2,1)S(1)}, bf16[384,768]{1,0:T(8,128)(2,1)S(1)...) custom-call(f32[192,768]{1,0:T(8,128)} %bitcast.13, ...), custom_call_target="tpu_custom_call" | custom-call | flops 6000000000 | bytes 1048576 | tf_op jit(solution)/shard_map/pallas_call | solution.py:267
  45.3 0.0 slice-start.1
  45.3 6.5 %shard_map.61 = (f32[576,256]{1,0:T(8,128)S(1)}, bf16[576,256]{1,0:T(8,128)(2,1)S(1)}, bf16[576,256]{1,0:T(8,128)(2,1)S(1)}, bf16[256,768]{1,0:T(8,128)(2,1)S(1)...) custom-call(f32[768,768]{1,0:T(8,128)S(1)} %get-tuple-element.27.refs_0_, ...), custom_call_target="tpu_custom_call" | custom-call | flops 4000000000 | bytes 1048576 | tf_op jit(solution)/shard_map/pallas_call | solution.py:267
  51.9 0.8 copy-done.2
  52.7 3.4 %collective-permute-start.7 = (bf16[576,256]{1,0:T(8,128)(2,1)S(1)}, bf16[576,256]{1,0:T(8,128)(2,1)S(1)}, u32[]{:S(2)}, u32[]{:S(2)}) collective-permute-start(bf16[576,256]{1,0:T(8,128)(2,1)S(1)} %get-tuple-element.32.refs_8_.refs_0_), channel_id=1, source_target_pairs={{0,2},{1,3},{2,0},{3,1},{4,6},{5,7},{6,4},{7,5},{8,10},{9,11},{10,... | collective-permute-start | bytes 884744 | tf_op jit(solution)/shard_map/ppermute | solution.py:18
  56.1 4.0 %shard_map.62 = (f32[576,128]{1,0:T(8,128)S(1)}, bf16[576,128]{1,0:T(8,128)(2,1)S(1)}, bf16[576,128]{1,0:T(8,128)(2,1)}) custom-call(f32[768,768]{1,0:T(8,128)S(1)} %get-tuple-element.27.refs_0_, f32[576,768]{1,0:T(8,128)S(1)} %get-tuple-element.28.refs_1_, bf16[576,384]{1,0:T(8,128)(2,1)S(1)} %get-tuple-element.23.refs_1_.refs_2_, ...), custom_call_target="tpu_custom_call" | custom-call | flops 2000000000 | bytes 1048576 | tf_op jit(solution)/shard_map/pallas_call | solution.py:267
  60.0 0.7 copy-done.4
  60.7 0.0 collective-permute-start.10
  60.8 0.7 collective-permute-start.9
  61.4 5.6 %collective-permute-done.10.refs_6_ = bf16[576,128]{1,0:T(8,128)(2,1)S(1)} collective-permute-done((bf16[576,128]{1,0:T(8,128)(2,1)S(1)}, bf16[576,128]{1,0:T(8,128)(2,1)S(1)}, u32[]{:S(2)}, u32[]{:S(2)}) %collective-permute-start.10) | collective-permute-done | bytes 147488 | tf_op jit(solution)/shard_map/ppermute | solution.py:18
  67.0 1.5 %collective-permute-start.6 = (bf16[576,256]{1,0:T(8,128)(2,1)S(1)}, bf16[576,256]{1,0:T(8,128)(2,1)S(1)}, u32[]{:S(2)}, u32[]{:S(2)}) collective-permute-start(bf16[576,256]{1,0:T(8,128)(2,1)S(1)} %get-tuple-element.32.refs_8_.refs_0_), channel_id=1, source_target_pairs={{0,1},{1,0},{2,3},{3,2},{4,5},{5,4},{6,7},{7,6},{8,9},{9,8},{10,11... | collective-permute-start | bytes 884744 | tf_op jit(solution)/shard_map/ppermute | solution.py:18
  68.5 0.0 collective-permute-done.3.refs_2_
  68.5 0.0 collective-permute-start.11
  68.5 0.0 collective-permute-done.7.refs_2_
  68.5 0.5 collective-permute-start.8
  69.0 0.0 collective-permute-done.5.refs_4_
  69.1 6.3 %shard_map.66.w_ref = f32[4,576,576]{2,1,0:T(8,128)S(1)} custom-call(f32[576,2304]{1,0:T(8,128)S(1)} %bitcast.10, bf16[576,384]{1,0:T(8,128)(2,1)S(1)} %get-tuple-element.23.refs_1_.refs_2_, f32[576,384]{1,0:T(8,128)S(1)} %collective-permute-done.3.refs_2_, f32[576,384]{1,0:T(8,128)S(1)} %collective-permute-done.4.refs_3_, ...), custom_call_target="tpu_custom_call" | custom-call | flops 8000000000 | bytes 1048576 | tf_op jit(solution)/shard_map/pallas_call | solution.py:368
  75.4 1.7 %shard_map.67 = bf16[576,576]{1,0:T(8,128)(2,1)} custom-call(f32[4,576,576]{2,1,0:T(8,128)S(1)} %shard_map.66.w_ref, bf16[576,256]{1,0:T(8,128)(2,1)S(1)} %get-tuple-element.32.refs_8_.refs_0_, bf16[576,256]{1,0:T(8,128)(2,1)S(1)} %collective-permute-done.6.refs_1_, bf16[576,256]{1,0:T(8,128)(2,1)S(1)} %collective-permute-done.7.refs_2_, ...), custom_call_target="tpu_custom_call" | custom-call | flops 500000000 | bytes 1048576 | tf_op jit(solution)/shard_map/pallas_call | solution.py:415
  77.1 3.6 %collective-permute-start.14 = (bf16[576,576]{1,0:T(8,128)(2,1)}, bf16[576,576]{1,0:T(8,128)(2,1)}, u32[]{:S(2)}, u32[]{:S(2)}) collective-permute-start(bf16[576,576]{1,0:T(8,128)(2,1)} %shard_map.67), channel_id=1, source_target_pairs={{0,12},{4,8},{8,4},{12,0},{16,28},{20,24},{24,20},{28,16},{32,44},... | collective-permute-start | bytes 1990664 | tf_op jit(solution)/shard_map/ppermute | solution.py:18
  80.6 8.7 %shard_map.60.w_ref = f32[4,576,576]{2,1,0:T(8,128)S(1)} custom-call(f32[576,2304]{1,0:T(8,128)S(1)} %bitcast.11, bf16[576,384]{1,0:T(8,128)(2,1)S(1)} %get-tuple-element.23.refs_1_.refs_2_, f32[576,384]{1,0:T(8,128)S(1)} %collective-permute-done.3.refs_2_, f32[576,384]{1,0:T(8,128)S(1)} %collective-permute-done.4.refs_3_, ...), custom_call_target="tpu_custom_call" | custom-call | flops 8000000000 | bytes 1048576 | tf_op jit(solution)/shard_map/pallas_call | solution.py:368
  89.3 2.2 %shard_map.65 = bf16[576,576]{1,0:T(8,128)(2,1)} custom-call(f32[4,576,576]{2,1,0:T(8,128)S(1)} %shard_map.60.w_ref, bf16[576,256]{1,0:T(8,128)(2,1)S(1)} %get-tuple-element.32.refs_8_.refs_0_, bf16[576,256]{1,0:T(8,128)(2,1)S(1)} %collective-permute-done.6.refs_1_, bf16[576,256]{1,0:T(8,128)(2,1)S(1)} %collective-permute-done.7.refs_2_, ...), custom_call_target="tpu_custom_call" | custom-call | flops 500000000 | bytes 1048576 | tf_op jit(solution)/shard_map/pallas_call | solution.py:415
  91.5 0.5 collective-permute-start.13
  91.9 0.1 copy-done
  92.1 1.7 %shard_map.64 = bf16[576,576]{1,0:T(8,128)(2,1)} custom-call(f32[4,576,576]{2,1,0:T(8,128)S(1)} %shard_map.60.w_ref, bf16[576,256]{1,0:T(8,128)(2,1)S(1)} %get-tuple-element.32.refs_8_.refs_0_, bf16[576,256]{1,0:T(8,128)(2,1)S(1)} %collective-permute-done.6.refs_1_, bf16[576,256]{1,0:T(8,128)(2,1)S(1)} %collective-permute-done.7.refs_2_, ...), custom_call_target="tpu_custom_call" | custom-call | flops 500000000 | bytes 1048576 | tf_op jit(solution)/shard_map/pallas_call | solution.py:415
  93.7 0.5 collective-permute-start.12
  94.2 1.2 dynamic-slice_subtract_fusion
  95.4 2.7 %copy-done.1 = f32[4,576,576]{2,1,0:T(8,128)S(1)} copy-done((f32[4,576,576]{2,1,0:T(8,128)S(1)}, f32[4,576,576]{2,1,0:T(8,128)}, u32[]{:S(2)}) %copy-start.1) | copy-done | bytes 5308440
  98.1 1.1 copy-done.3
  99.2 1.0 copy-done.5
  100.1 1.4 shard_map.63
  101.5 1.3 shard_map.68.refs_3_
  102.9 2.6 %shard_map.69.refs_3_ = f32[768,768]{1,0:T(8,128)S(1)} custom-call(bf16[576,576]{1,0:T(8,128)(2,1)} %collective-permute-done.14.refs_0_, s32[1,576]{1,0:T(1,128)S(1)} %get-tuple-element.46.refs_1_, s32[1,576]{1,0:T(1,128)S(1)} %get-tuple-element.45.refs_2_, f32[768,768]{1,0:T(8,128)S(1)} %shard_map.68.refs_3_), custom_call_target="tpu_custom_call", output_to_operand_aliasing={{}: (3, {})} | custom-call | flops 679477248 | bytes 1048576 | tf_op jit(solution)/shard_map/pallas_call | solution.py:479
  105.4 9.1 %collective-permute-done.13.refs_0_ = bf16[576,576]{1,0:T(8,128)(2,1)} collective-permute-done((bf16[576,576]{1,0:T(8,128)(2,1)}, bf16[576,576]{1,0:T(8,128)(2,1)}, u32[]{:S(2)}, u32[]{:S(2)}) %collective-permute-start.13) | collective-permute-done | bytes 663584 | tf_op jit(solution)/shard_map/ppermute | solution.py:18
  114.6 2.6 %shard_map.70.refs_3_ = f32[768,768]{1,0:T(8,128)S(1)} custom-call(bf16[576,576]{1,0:T(8,128)(2,1)} %collective-permute-done.13.refs_0_, s32[1,576]{1,0:T(1,128)S(1)} %get-tuple-element.48.refs_1_, s32[1,576]{1,0:T(1,128)S(1)} %get-tuple-element.47.refs_2_, f32[768,768]{1,0:T(8,128)S(1)} %shard_map.69.refs_3_), custom_call_target="tpu_custom_call", output_to_operand_aliasing={{}: (3, {})} | custom-call | flops 679477248 | bytes 1048576 | tf_op jit(solution)/shard_map/pallas_call | solution.py:479
  117.2 27.3 %collective-permute-done.12.refs_0_ = bf16[576,576]{1,0:T(8,128)(2,1)S(1)} collective-permute-done((bf16[576,576]{1,0:T(8,128)(2,1)}, bf16[576,576]{1,0:T(8,128)(2,1)S(1)}, u32[]{:S(2)}, u32[]{:S(2)}) %collective-permute-start.12) | collective-permute-done | bytes 663584 | tf_op jit(solution)/shard_map/ppermute | solution.py:18
  144.5 2.4 %shard_map.71 = f32[768,1,768]{2,1,0:T(1,128)} custom-call(bf16[576,576]{1,0:T(8,128)(2,1)S(1)} %collective-permute-done.12.refs_0_, s32[1,576]{1,0:T(1,128)S(1)} %get-tuple-element.50.refs_1_, s32[1,576]{1,0:T(1,128)S(1)} %get-tuple-element.49.refs_2_, f32[768,768]{1,0:T(8,128)S(1)} %shard_map.70.refs_3_), custom_call_target="tpu_custom_call" | custom-call | flops 679477248 | bytes 1048576 | tf_op jit(solution)/shard_map/pallas_call | solution.py:479
  (17 shorter events, 0.0 us)
Async XLA Ops:
  0.6 6.9 %copy-start.6 = (f32[1,192,768]{2,1,0:T(8,128)S(1)}, f32[1,192,768]{2,1,0:T(8,128)}, u32[]{:S(2)}) copy-start(f32[1,192,768]{2,1,0:T(8,128)} %param.4) | copy-start | bytes 1769476
  2.8 30.7 %collective-permute-start.4 = (f32[576,384]{1,0:T(8,128)}, f32[576,384]{1,0:T(8,128)S(1)}, u32[]{:S(2)}, u32[]{:S(2)}) collective-permute-start(f32[576,384]{1,0:T(8,128)} %slice_bitcast_fusion), channel_id=1, source_target_pairs={{0,2},{1,3},{2,0},{3,1},{4,6},{5,7},{6,4},{7,5},{8,10},{9,11},{10,... | collective-permute-start | bytes 2654216 | tf_op jit(solution)/shard_map/ppermute | solution.py:18
  7.4 23.9 %collective-permute-start.1 = (f32[192,384]{1,0:T(8,128)S(1)}, f32[192,384]{1,0:T(8,128)S(1)}, u32[]{:S(2)}, u32[]{:S(2)}) collective-permute-start(f32[192,384]{1,0:T(8,128)S(1)} %dynamic-slice_bitcast_fusion), channel_id=1, source_target_pairs={{0,2},{1,3},{2,0},{3,1},{4,6},{5,7},{6,4},{7,5},{8,10},{9,11},{10,... | collective-permute-start | bytes 884744 | tf_op jit(solution)/shard_map/ppermute | solution.py:18
  7.5 27.2 %collective-permute-start = (f32[192,768]{1,0:T(8,128)S(1)}, f32[192,768]{1,0:T(8,128)S(1)}, u32[]{:S(2)}, u32[]{:S(2)}) collective-permute-start(f32[192,768]{1,0:T(8,128)S(1)} %bitcast.14), channel_id=1, source_target_pairs={{0,1},{1,0},{2,3},{3,2},{4,5},{5,4},{6,7},{7,6},{8,9},{9,8},{10,11... | collective-permute-start | bytes 1769480 | tf_op jit(solution)/shard_map/ppermute | solution.py:18
  31.3 3.5 %collective-permute-start.2 = (f32[192,384]{1,0:T(8,128)S(1)}, f32[192,384]{1,0:T(8,128)S(1)}, u32[]{:S(2)}, u32[]{:S(2)}) collective-permute-start(f32[192,384]{1,0:T(8,128)S(1)} %collective-permute-done.1.refs_2_), channel_id=1, source_target_pairs={{0,1},{1,0},{2,3},{3,2},{4,5},{5,4},{6,7},{7,6},{8,9},{9,8},{10,11... | collective-permute-start | bytes 884744 | tf_op jit(solution)/shard_map/ppermute | solution.py:18
  33.5 35.0 %collective-permute-start.3 = (f32[576,384]{1,0:T(8,128)}, f32[576,384]{1,0:T(8,128)S(1)}, u32[]{:S(2)}, u32[]{:S(2)}) collective-permute-start(f32[576,384]{1,0:T(8,128)} %slice_bitcast_fusion), channel_id=1, source_target_pairs={{0,1},{1,0},{2,3},{3,2},{4,5},{5,4},{6,7},{7,6},{8,9},{9,8},{10,11... | collective-permute-start | bytes 2654216 | tf_op jit(solution)/shard_map/ppermute | solution.py:18
  33.5 35.5 %collective-permute-start.5 = (f32[576,384]{1,0:T(8,128)S(1)}, f32[576,384]{1,0:T(8,128)S(1)}, u32[]{:S(2)}, u32[]{:S(2)}) collective-permute-start(f32[576,384]{1,0:T(8,128)S(1)} %collective-permute-done.4.refs_3_), channel_id=1, source_target_pairs={{0,1},{1,0},{2,3},{3,2},{4,5},{5,4},{6,7},{7,6},{8,9},{9,8},{10,11... | collective-permute-start | bytes 2654216 | tf_op jit(solution)/shard_map/ppermute | solution.py:18
  34.7 34.3 %slice-start = ((s8[5308416]{0:T(1024)(128)(4,1)}), s8[4194304]{0:T(1024)(128)(4,1)S(1)}, s32[]{:S(2)}) async-start(s8[5308416]{0:T(1024)(128)(4,1)} %bitcast.8), calls=%async_computation | async-start | bytes 8388608
  45.3 23.7 %slice-start.1 = ((s8[5308416]{0:T(1024)(128)(4,1)}), s8[1114112]{0:T(1024)(128)(4,1)S(1)}, s32[]{:S(2)}) async-start(s8[5308416]{0:T(1024)(128)(4,1)} %bitcast.8), calls=%async_computation.1 | async-start | bytes 2228224
  51.9 0.8 copy-start.2
  52.7 15.8 %collective-permute-start.7 = (bf16[576,256]{1,0:T(8,128)(2,1)S(1)}, bf16[576,256]{1,0:T(8,128)(2,1)S(1)}, u32[]{:S(2)}, u32[]{:S(2)}) collective-permute-start(bf16[576,256]{1,0:T(8,128)(2,1)S(1)} %get-tuple-element.32.refs_8_.refs_0_), channel_id=1, source_target_pairs={{0,2},{1,3},{2,0},{3,1},{4,6},{5,7},{6,4},{7,5},{8,10},{9,11},{10,... | collective-permute-start | bytes 884744 | tf_op jit(solution)/shard_map/ppermute | solution.py:18
  60.0 0.7 copy-start.4
  60.7 6.3 %collective-permute-start.10 = (bf16[576,128]{1,0:T(8,128)(2,1)S(1)}, bf16[576,128]{1,0:T(8,128)(2,1)S(1)}, u32[]{:S(2)}, u32[]{:S(2)}) collective-permute-start(bf16[576,128]{1,0:T(8,128)(2,1)S(1)} %get-tuple-element.38.refs_4_), channel_id=1, source_target_pairs={{0,2},{1,3},{2,0},{3,1},{4,6},{5,7},{6,4},{7,5},{8,10},{9,11},{10,... | collective-permute-start | bytes 442376 | tf_op jit(solution)/shard_map/ppermute | solution.py:18
  60.8 14.6 %collective-permute-start.9 = (bf16[576,128]{1,0:T(8,128)(2,1)S(1)}, bf16[576,128]{1,0:T(8,128)(2,1)S(1)}, u32[]{:S(2)}, u32[]{:S(2)}) collective-permute-start(bf16[576,128]{1,0:T(8,128)(2,1)S(1)} %get-tuple-element.38.refs_4_), channel_id=1, source_target_pairs={{0,1},{1,0},{2,3},{3,2},{4,5},{5,4},{6,7},{7,6},{8,9},{9,8},{10,11... | collective-permute-start | bytes 442376 | tf_op jit(solution)/shard_map/ppermute | solution.py:18
  67.0 8.4 %collective-permute-start.6 = (bf16[576,256]{1,0:T(8,128)(2,1)S(1)}, bf16[576,256]{1,0:T(8,128)(2,1)S(1)}, u32[]{:S(2)}, u32[]{:S(2)}) collective-permute-start(bf16[576,256]{1,0:T(8,128)(2,1)S(1)} %get-tuple-element.32.refs_8_.refs_0_), channel_id=1, source_target_pairs={{0,1},{1,0},{2,3},{3,2},{4,5},{5,4},{6,7},{7,6},{8,9},{9,8},{10,11... | collective-permute-start | bytes 884744 | tf_op jit(solution)/shard_map/ppermute | solution.py:18
  68.5 6.9 %collective-permute-start.11 = (bf16[576,128]{1,0:T(8,128)(2,1)S(1)}, bf16[576,128]{1,0:T(8,128)(2,1)S(1)}, u32[]{:S(2)}, u32[]{:S(2)}) collective-permute-start(bf16[576,128]{1,0:T(8,128)(2,1)S(1)} %collective-permute-done.10.refs_6_), channel_id=1, source_target_pairs={{0,1},{1,0},{2,3},{3,2},{4,5},{5,4},{6,7},{7,6},{8,9},{9,8},{10,11... | collective-permute-start | bytes 442376 | tf_op jit(solution)/shard_map/ppermute | solution.py:18
  68.5 6.9 %collective-permute-start.8 = (bf16[576,256]{1,0:T(8,128)(2,1)S(1)}, bf16[576,256]{1,0:T(8,128)(2,1)S(1)}, u32[]{:S(2)}, u32[]{:S(2)}) collective-permute-start(bf16[576,256]{1,0:T(8,128)(2,1)S(1)} %collective-permute-done.7.refs_2_), channel_id=1, source_target_pairs={{0,1},{1,0},{2,3},{3,2},{4,5},{5,4},{6,7},{7,6},{8,9},{9,8},{10,11... | collective-permute-start | bytes 884744 | tf_op jit(solution)/shard_map/ppermute | solution.py:18
  77.1 25.8 %collective-permute-start.14 = (bf16[576,576]{1,0:T(8,128)(2,1)}, bf16[576,576]{1,0:T(8,128)(2,1)}, u32[]{:S(2)}, u32[]{:S(2)}) collective-permute-start(bf16[576,576]{1,0:T(8,128)(2,1)} %shard_map.67), channel_id=1, source_target_pairs={{0,12},{4,8},{8,4},{12,0},{16,28},{20,24},{24,20},{28,16},{32,44},... | collective-permute-start | bytes 1990664 | tf_op jit(solution)/shard_map/ppermute | solution.py:18
  89.3 2.7 %copy-start = (f32[4,576,576]{2,1,0:T(8,128)}, f32[4,576,576]{2,1,0:T(8,128)S(1)}, u32[]{:S(2)}) copy-start(f32[4,576,576]{2,1,0:T(8,128)S(1)} %shard_map.60.w_ref) | copy-start | bytes 15925252
  91.5 23.1 %collective-permute-start.13 = (bf16[576,576]{1,0:T(8,128)(2,1)}, bf16[576,576]{1,0:T(8,128)(2,1)}, u32[]{:S(2)}, u32[]{:S(2)}) collective-permute-start(bf16[576,576]{1,0:T(8,128)(2,1)} %shard_map.65), channel_id=1, source_target_pairs={{0,4},{4,0},{8,12},{12,8},{16,20},{20,16},{24,28},{28,24},{32,36},... | collective-permute-start | bytes 1990664 | tf_op jit(solution)/shard_map/ppermute | solution.py:18
  93.7 50.7 %collective-permute-start.12 = (bf16[576,576]{1,0:T(8,128)(2,1)}, bf16[576,576]{1,0:T(8,128)(2,1)S(1)}, u32[]{:S(2)}, u32[]{:S(2)}) collective-permute-start(bf16[576,576]{1,0:T(8,128)(2,1)} %shard_map.64), channel_id=1, source_target_pairs={{0,8},{4,12},{8,0},{12,4},{16,24},{20,28},{24,16},{28,20},{32,40},... | collective-permute-start | bytes 1990664 | tf_op jit(solution)/shard_map/ppermute | solution.py:18
  95.4 2.7 %copy-start.1 = (f32[4,576,576]{2,1,0:T(8,128)S(1)}, f32[4,576,576]{2,1,0:T(8,128)}, u32[]{:S(2)}) copy-start(f32[4,576,576]{2,1,0:T(8,128)} %copy-done) | copy-start | bytes 15925252
  98.1 1.1 copy-start.3
  99.2 1.0 copy-start.5
